TPU v7x, 256 devices: a whole 4x4x8 slice. The times are simulated.
256 devices in a mesh: pair: 2 (over y_hi), grp: 8 (over z), seq: 16 (over y_lo, x, core).
Axes of the slice: x: 4, y: 4 (y_hi: 2, y_lo: 2; y = y_hi * 2 + y_lo), z: 8, core: 2. Of those that a mesh axis runs over, the one named last changes fastest.
Arguments:
- series: float32 [8, 32768, 64], P('grp', 'seq', 'pair'), may hold values from -8 to 8
- time_blocks: int32 [8, 16], P('grp'), may hold values from 0 to 127
- freq_blocks: int32 [8, 16], P('grp'), may hold values from 0 to 127
- positives: int32 [8], replicated, may hold values from 0 to 7, each once
- conv_weight: bfloat16 [2, 1024, 512], P('pair'), may hold values from -0.25 to 0.25
- proj_weight: bfloat16 [2, 1024, 128], P('pair'), may hold values from -0.1875 to 0.1875
Outputs:
- encoded: bfloat16 [2, 8, 16384, 1024], P('pair', 'grp', 'seq')
- loss_value: float32 [], replicated
- grad_conv: float32 [2, 1024, 512], P('pair', ('grp', 'seq'))
- grad_proj: float32 [2, 1024, 128], P('pair', 'grp')
Inputs may be any that keep to these rules, and one draw needn't show every extreme that they name: `positives`: each of 0 to 7 stands once.
All inputs are finite; a program needn't handle non-finite values.
Results may differ from a plain program's by a relative error of at most 0.0042.
Values may be sent and summed in bfloat16 or wider, within the bound.
A program may use at most 128 MiB of HBM per device.

v0:
```python
import math

import jax
import jax.numpy as jnp
from jax import lax
from jax.sharding import PartitionSpec as P

C = 64
H = 1024
K = 8


TAU = 0.2
LOSS_SCALE = 256.0


def from_partner(value, axis, distance):
    mask = 2**distance
    pairs = [(source, source ^ mask) for source in range(lax.axis_size(axis))]
    return lax.ppermute(value, axis, pairs)


def extended(block, sides, width):
    for axis, dim in sides:
        count = lax.axis_size(axis)
        forward = [(i, i + 1) for i in range(count - 1)]
        backward = [(target, source) for source, target in forward]
        low = lax.ppermute(
            lax.slice_in_dim(block, block.shape[dim] - width, None, axis=dim), axis, forward
        )
        high = lax.ppermute(lax.slice_in_dim(block, 0, width, axis=dim), axis, backward)
        block = jnp.concatenate([low, block, high], axis=dim)
    return block


def gelu_slope(values):
    output, pullback = jax.vjp(lambda argument: jax.nn.gelu(argument, approximate=True), values)
    return (output, pullback(jnp.ones_like(values))[0])


def embed(pooled, projection):
    latent = jnp.dot(pooled, projection, precision=lax.Precision.HIGHEST)
    return latent * lax.rsqrt(jnp.sum(latent * latent, axis=1, keepdims=True) + 1e-06)


def contrast(time_emb, freq_emb, positives):
    logits = jnp.dot(time_emb, freq_emb.T, precision=lax.Precision.HIGHEST) / TAU
    number = logits.shape[0]
    target = (positives[:, None] == jnp.arange(number, dtype=jnp.int32)[None, :]).astype(
        logits.dtype
    )
    exponent = jnp.exp(logits)
    row_lse = jnp.log(jnp.sum(exponent, axis=1))
    col_lse = jnp.log(jnp.sum(exponent, axis=0))
    picked = jnp.sum(target * logits)
    return (jnp.sum(row_lse) + jnp.sum(col_lse) - 2.0 * picked) / (2.0 * number)


def body(series, time_blocks, freq_blocks, positives, conv_weight, proj_weight):
    groups = lax.axis_size("seq")
    seq_pos = lax.axis_index("seq")
    branch = lax.axis_index("pair")
    grp_pos = lax.axis_index("grp")
    samples, length, own_chan = series.shape
    block_len = length // groups
    full_len = length * groups
    highest = lax.Precision.HIGHEST
    flat_in = series.reshape(samples, groups, block_len * own_chan)
    arrived = lax.all_to_all(flat_in, "seq", split_axis=1, concat_axis=1, tiled=True)
    source = jnp.arange(groups, dtype=jnp.int32)
    small_phases = source[:, None] * source[None, :] % groups
    small_angles = small_phases.astype(jnp.float32) * (2.0 * math.pi / groups)
    part_re = jnp.einsum("rs,bsj->brj", jnp.cos(small_angles), arrived, precision=highest)
    part_im = -jnp.einsum("rs,bsj->brj", jnp.sin(small_angles), arrived, precision=highest)
    local_steps = seq_pos * block_len + jnp.arange(block_len, dtype=jnp.int32)
    twist = source[:, None] * local_steps[None, :] % full_len
    twist_angles = twist.astype(jnp.float32) * (2.0 * math.pi / full_len)
    twist_cos = jnp.cos(twist_angles)[None, :, :, None]
    twist_sin = jnp.sin(twist_angles)[None, :, :, None]
    part_re = part_re.reshape(samples, groups, block_len, own_chan)
    part_im = part_im.reshape(samples, groups, block_len, own_chan)
    turned_re = (part_re * twist_cos + part_im * twist_sin).reshape(
        samples, groups, block_len * own_chan
    )
    turned_im = (part_im * twist_cos - part_re * twist_sin).reshape(
        samples, groups, block_len * own_chan
    )
    strided_re, strided_im = (
        lax.all_to_all(turned_re, "seq", split_axis=1, concat_axis=2, tiled=True),
        lax.all_to_all(turned_im, "seq", split_axis=1, concat_axis=2, tiled=True),
    )
    stacked = jnp.concatenate(
        [
            strided_re.reshape(samples, length, own_chan),
            strided_im.reshape(samples, length, own_chan),
        ],
        axis=2,
    )
    out_block = min(256, length)
    step_ids = jnp.arange(length, dtype=jnp.int32)

    def fourier_block(block_id):
        rows_idx = block_id * out_block + jnp.arange(out_block, dtype=jnp.int32)
        phases = rows_idx[:, None] * step_ids[None, :] % length
        angles = phases.astype(jnp.float32) * (2.0 * math.pi / length)
        cos_part = jnp.einsum("jm,smc->sjc", jnp.cos(angles), stacked, precision=highest)
        sin_part = jnp.einsum("jm,smc->sjc", jnp.sin(angles), stacked, precision=highest)
        return (
            cos_part[..., :own_chan] + sin_part[..., own_chan:],
            cos_part[..., own_chan:] - sin_part[..., :own_chan],
        )

    blocks_re, blocks_im = lax.map(fourier_block, jnp.arange(length // out_block, dtype=jnp.int32))
    spec_re = jnp.moveaxis(blocks_re, 0, 1).reshape(samples, length, own_chan)
    spec_im = jnp.moveaxis(blocks_im, 0, 1).reshape(samples, length, own_chan)
    bins_re, bins_im = (
        lax.all_to_all(
            spec_re.reshape(samples, groups, block_len, 1, own_chan),
            "seq",
            split_axis=1,
            concat_axis=3,
            tiled=True,
        ),
        lax.all_to_all(
            spec_im.reshape(samples, groups, block_len, 1, own_chan),
            "seq",
            split_axis=1,
            concat_axis=3,
            tiled=True,
        ),
    )
    bins_re = bins_re.reshape(samples, length, own_chan)
    bins_im = bins_im.reshape(samples, length, own_chan)
    freq_own = jnp.sqrt(1.0 + (bins_re * bins_re + bins_im * bins_im) / full_len).astype(
        jnp.bfloat16
    )
    time_own = series.astype(jnp.bfloat16)
    is_time = branch == 0
    own_feat = jnp.where(is_time, time_own, freq_own)
    payload = jnp.where(is_time, freq_own, time_own)
    received = from_partner(payload, "pair", 0)
    inputs = jnp.concatenate(
        [jnp.where(is_time, own_feat, received), jnp.where(is_time, received, own_feat)], axis=2
    )
    chosen = jnp.where(is_time, time_blocks, freq_blocks)
    position = seq_pos * length + jnp.arange(length, dtype=jnp.int32)
    block_ids = position // (length // 8)
    listed = jnp.any(chosen[:, :, None] == block_ids[None, None, :], axis=1)
    inputs = inputs * jnp.where(listed, 0.0, 1.0).astype(jnp.bfloat16)[:, :, None]
    padded = extended(inputs, (("seq", 1),), K // 2)
    patches = jnp.concatenate([padded[:, offset : offset + length] for offset in range(K)], axis=2)
    flat_patch = patches.reshape(samples * length, K * C)
    weight = conv_weight[0]
    step_rows = min(512, length)
    per_sample = length // step_rows
    block_count = samples * per_sample

    def forward_block(block_id):
        patch_rows = lax.dynamic_slice_in_dim(flat_patch, block_id * step_rows, step_rows, 0)
        preact = lax.dot_general(
            patch_rows, weight, (((1,), (1,)), ((), ())), preferred_element_type=jnp.float32
        )
        active, slopes = gelu_slope(preact)
        pairs = active.reshape(step_rows // 2, 2, active.shape[1])
        halved = ((pairs[:, 0] + pairs[:, 1]) * 0.5).astype(jnp.bfloat16)
        return (halved, jnp.sum(active, axis=0), slopes)

    halved_all, block_sums, slopes_all = lax.map(
        forward_block, jnp.arange(block_count, dtype=jnp.int32)
    )
    encoded = halved_all.reshape(samples, length // 2, H)
    local_sum = block_sums.reshape(samples, per_sample, H).sum(axis=1)
    pooled = lax.psum(local_sum, "seq") / full_len
    projection = proj_weight[0].astype(jnp.float32)
    own_emb = embed(pooled, projection)
    gathered = lax.all_gather(own_emb, "grp", axis=0, tiled=True)
    partner = from_partner(gathered, "pair", 0)
    time_emb = jnp.where(is_time, gathered, partner)
    freq_emb = jnp.where(is_time, partner, gathered)
    loss_value, emb_grads = jax.value_and_grad(contrast, argnums=(0, 1))(
        time_emb, freq_emb, positives
    )
    own_grad = jnp.where(is_time, emb_grads[0], emb_grads[1])
    own_grad = lax.dynamic_slice_in_dim(own_grad, grp_pos * samples, samples, 0)
    _, pullback = jax.vjp(embed, pooled, projection)
    pooled_grad, proj_grad = pullback(own_grad * LOSS_SCALE)
    proj_share = lax.psum_scatter(proj_grad, "grp", scatter_dimension=0, tiled=True)
    scaled = pooled_grad / full_len

    def accumulate(running, block_id):
        patch_rows = lax.dynamic_slice_in_dim(flat_patch, block_id * step_rows, step_rows, 0)
        slopes = lax.dynamic_index_in_dim(slopes_all, block_id, 0, keepdims=False)
        factor = lax.dynamic_index_in_dim(scaled, block_id // per_sample, 0, keepdims=False)
        upstream = (factor[None, :] * slopes).astype(jnp.bfloat16)
        update = lax.dot_general(
            upstream, patch_rows, (((0,), (0,)), ((), ())), preferred_element_type=jnp.float32
        )
        return (running + update, None)

    result, _ = lax.scan(
        accumulate,
        jnp.zeros(
            (H // (lax.axis_size("grp") * groups) * lax.axis_size(("grp", "seq")), K * C),
            jnp.float32,
        ),
        jnp.arange(block_count, dtype=jnp.int32),
    )
    conv_share = lax.psum_scatter(result, ("grp", "seq"), scatter_dimension=0, tiled=True)
    return (encoded[None], loss_value, conv_share[None], proj_share[None])


def solution(mesh):
    in_specs = (
        P("grp", "seq", "pair"),
        P("grp", None),
        P("grp", None),
        P(),
        P("pair", None, None),
        P("pair", None, None),
    )
    out_specs = (
        P("pair", "grp", "seq", None),
        P(),
        P("pair", ("grp", "seq"), None),
        P("pair", "grp", None),
    )
    return jax.shard_map(body, mesh=mesh, in_specs=in_specs, out_specs=out_specs, check_vma=False)
```

profile of v0, /device:TPU:1, one launch (start us, length us, event | category | flops | bytes accessed | tf_op | source)
XLA Modules:
  0.0 1055.2 jit_solution(11123865440484076041)
XLA Ops:
  9.7 6.8 all-to-all-start
  18.2 5.5 all-to-all-done
  25.7 4.1 all-to-all-start.1
  30.7 6.3 all-to-all-done.1
  37.0 4.1 all-to-all-start.2
  42.1 6.3 all-to-all-done.2
  52.3 216.7 %while.43 = (s32[]{:T(128)}, f32[8,1,256,32]{2,0,3,1:T(8,128)}, f32[8,1,256,32]{2,0,3,1:T(8,128)}, s32[8]{0:T(128)S(1)}, f32[1,2048,64]{2,1,0:T(8,128)}, /*index=5*/s32[]{:T(128)}, s32[1]{0:T(128)}, s32[]{:T(128)}) while((s32[]{:T(128)}, f32[8,1,256,32]{2,0,3,1:T(8,128)}, f32[8,1,256,32]{2,0,3,1:T(8,128)}, s32[8]{0:T(128)S(1)}, ...), condition=%wide.region_1.2_spmd.clone, body=%wide.region_0.1_spmd.clone.sunk | while | flops 820003072 | bytes 3738773 | solution.py:113
  66.9 11.0 %fusion.147 = f32[1,256,64]{1,2,0:T(8,128)S(1)} fusion(f32[1,2048,64]{2,1,0:T(8,128)} %get-tuple-element.464, s32[256]{0:T(256)S(1)} %iota_add_fusion.4), kind=kOutput, calls=%fused_computation.35.clone.1 | convolution fusion | flops 409993216 | bytes 590848 | tf_op jit(solution)/shard_map/while/body/eval_jaxpr/jm,smc->sjc/dot_general | solution.py:107
  77.9 9.6 fusion.148
  87.6 1.8 dynamic_update_slice.47
  92.3 11.0 %fusion.147 = f32[1,256,64]{1,2,0:T(8,128)S(1)} fusion(f32[1,2048,64]{2,1,0:T(8,128)} %get-tuple-element.464, s32[256]{0:T(256)S(1)} %iota_add_fusion.4), kind=kOutput, calls=%fused_computation.35.clone.1 | convolution fusion | flops 409993216 | bytes 590848 | tf_op jit(solution)/shard_map/while/body/eval_jaxpr/jm,smc->sjc/dot_general | solution.py:107
  103.3 9.6 fusion.148
  113.0 1.8 dynamic_update_slice.47
  117.8 11.0 %fusion.147 = f32[1,256,64]{1,2,0:T(8,128)S(1)} fusion(f32[1,2048,64]{2,1,0:T(8,128)} %get-tuple-element.464, s32[256]{0:T(256)S(1)} %iota_add_fusion.4), kind=kOutput, calls=%fused_computation.35.clone.1 | convolution fusion | flops 409993216 | bytes 590848 | tf_op jit(solution)/shard_map/while/body/eval_jaxpr/jm,smc->sjc/dot_general | solution.py:107
  128.7 9.6 fusion.148
  138.4 1.8 dynamic_update_slice.47
  143.2 11.0 %fusion.147 = f32[1,256,64]{1,2,0:T(8,128)S(1)} fusion(f32[1,2048,64]{2,1,0:T(8,128)} %get-tuple-element.464, s32[256]{0:T(256)S(1)} %iota_add_fusion.4), kind=kOutput, calls=%fused_computation.35.clone.1 | convolution fusion | flops 409993216 | bytes 590848 | tf_op jit(solution)/shard_map/while/body/eval_jaxpr/jm,smc->sjc/dot_general | solution.py:107
  154.2 9.6 fusion.148
  163.8 1.8 dynamic_update_slice.47
  168.6 11.0 %fusion.147 = f32[1,256,64]{1,2,0:T(8,128)S(1)} fusion(f32[1,2048,64]{2,1,0:T(8,128)} %get-tuple-element.464, s32[256]{0:T(256)S(1)} %iota_add_fusion.4), kind=kOutput, calls=%fused_computation.35.clone.1 | convolution fusion | flops 409993216 | bytes 590848 | tf_op jit(solution)/shard_map/while/body/eval_jaxpr/jm,smc->sjc/dot_general | solution.py:107
  179.6 9.6 fusion.148
  189.2 1.8 dynamic_update_slice.47
  194.0 11.0 %fusion.147 = f32[1,256,64]{1,2,0:T(8,128)S(1)} fusion(f32[1,2048,64]{2,1,0:T(8,128)} %get-tuple-element.464, s32[256]{0:T(256)S(1)} %iota_add_fusion.4), kind=kOutput, calls=%fused_computation.35.clone.1 | convolution fusion | flops 409993216 | bytes 590848 | tf_op jit(solution)/shard_map/while/body/eval_jaxpr/jm,smc->sjc/dot_general | solution.py:107
  205.0 9.6 fusion.148
  214.7 1.8 dynamic_update_slice.47
  219.4 11.0 %fusion.147 = f32[1,256,64]{1,2,0:T(8,128)S(1)} fusion(f32[1,2048,64]{2,1,0:T(8,128)} %get-tuple-element.464, s32[256]{0:T(256)S(1)} %iota_add_fusion.4), kind=kOutput, calls=%fused_computation.35.clone.1 | convolution fusion | flops 409993216 | bytes 590848 | tf_op jit(solution)/shard_map/while/body/eval_jaxpr/jm,smc->sjc/dot_general | solution.py:107
  230.4 9.6 fusion.148
  244.9 11.0 %fusion.147 = f32[1,256,64]{1,2,0:T(8,128)S(1)} fusion(f32[1,2048,64]{2,1,0:T(8,128)} %get-tuple-element.464, s32[256]{0:T(256)S(1)} %iota_add_fusion.4), kind=kOutput, calls=%fused_computation.35.clone.1 | convolution fusion | flops 409993216 | bytes 590848 | tf_op jit(solution)/shard_map/while/body/eval_jaxpr/jm,smc->sjc/dot_general | solution.py:107
  255.8 9.6 fusion.148
  265.5 1.8 dynamic_update_slice.47
  270.8 4.1 all-to-all-start.3
  276.7 5.5 all-to-all-done.3
  282.2 4.1 all-to-all-start.4
  286.5 7.0 all-to-all-done.4
  294.2 2.7 collective-permute-start
  296.9 11.6 %collective-permute-done = bf16[1,2048,32]{2,1,0:T(8,128)(2,1)S(1)} collective-permute-done((bf16[1,2048,32]{2,1,0:T(8,128)(2,1)S(1)}, bf16[1,2048,32]{2,1,0:T(8,128)(2,1)S(1)}, u32[]{:S(2)}, u32[]{:S(2)}) %collective-permute-start) | collective-permute-done | bytes 131104 | tf_op jit(solution)/shard_map/ppermute | solution.py:20
  309.2 3.7 collective-permute-start.1
  312.9 1.9 collective-permute-start.2
  314.8 2.9 collective-permute-done.2
  317.8 2.8 pad_maximum_fusion.1
  320.6 5.4 concatenate.33
  326.0 56.7 %while.42 = (s32[]{:T(128)}, bf16[4,256,1024]{2,1,0:T(8,128)(2,1)}, f32[4,1024]{1,0:T(4,128)S(1)}, f32[4,512,1024]{2,1,0:T(8,128)}, s32[4]{0:T(128)S(1)}, /*inde...) while((s32[]{:T(128)}, bf16[4,256,1024]{2,1,0:T(8,128)(2,1)}, ...), condition=%wide.region_5.6_spmd, body=%wide.region_3.5_spmd.sunk | while | flops 551287808 | bytes 46150916 | solution.py:168
  327.4 4.3 fusion.139
  331.7 2.5 reshape.444
  337.6 2.6 fusion.142
  341.6 4.3 fusion.139
  345.9 2.5 reshape.444
  351.8 2.5 fusion.142
  355.8 4.3 fusion.139
  360.0 2.5 reshape.444
  365.9 2.6 fusion.142
  369.9 4.3 fusion.139
  374.2 2.5 reshape.444
  380.1 2.6 fusion.142
  382.8 24.7 %psum.7 = f32[1,1024]{1,0:T(1,128)S(1)} all-reduce(f32[1,1024]{1,0:T(1,128)S(1)} %bitcast.158), channel_id=1, replica_groups=mesh['pair'=2,'grp'=8,'seq'=16] {'seq'}, use_global_device_ids=true, to_apply=%region_7.8 | all-reduce | flops 1024 | bytes 8192 | tf_op jit(solution)/shard_map/psum | solution.py:173
  409.0 15.4 %all-gather.1 = f32[8,1,128]{2,1,0:T(1,128)S(1)} all-gather(f32[1,1,128]{2,1,0:T(1,128)S(1)} %fusion.105), channel_id=2, replica_groups=mesh['pair'=2,'grp'=8,'seq'=16] {'grp'}, dimensions={0}, use_global_device_ids=true | all-gather | bytes 4608 | tf_op jit(solution)/shard_map/all_gather | solution.py:176
  424.4 2.6 collective-permute-start.3
  432.9 29.7 %while.44 = (s32[]{:T(128)}, f32[1024,512]{1,0:T(8,128)}, f32[1,1024]{1,0:T(1,128)S(1)}, s32[4]{0:T(128)S(1)}, f32[4,512,1024]{2,1,0:T(8,128)}, /*index=5*/bf16[...) while((s32[]{:T(128)}, f32[1024,512]{1,0:T(8,128)}, ...), condition=%wide.region_16.17_spmd.clone, body=%wide.region_15.16_spmd.clone.sunk | while | flops 538968064 | bytes 6820059 | solution.py:200
  436.1 3.7 select_add_fusion.2
  443.0 4.4 select_add_fusion.2
  450.6 4.4 select_add_fusion.2
  458.2 4.4 select_add_fusion.2
  464.4 8.8 reduce-scatter.5.cloned.1.call-done
  473.3 573.6 %reduce-scatter.3.cloned.1.call-done = f32[8,512]{1,0:T(8,128)} async-done(((f32[1024,512]{1,0:T(8,128)}), f32[8,512]{1,0:T(8,128)}) %reduce-scatter.3.cloned.1.call-update) | async-done | bytes 16400 | tf_op jit(solution)/shard_map/reduce_scatter | solution.py:208
  (176 shorter events, 63.0 us)
Async XLA Ops:
  7.2 400.3 %copy-start = (bf16[1,1024,128]{2,1,0:T(8,128)(2,1)S(1)}, bf16[1,1024,128]{2,1,0:T(8,128)(2,1)}, u32[]{:S(2)}) copy-start(bf16[1,1024,128]{2,1,0:T(8,128)(2,1)} %param.17) | copy-start | bytes 786436
  9.7 14.0 %all-to-all-start = ((f32[1,16,4096]{2,0,1:T(1,128)}), f32[1,16,4096]{2,0,1:T(1,128)S(1)}, u32[]{:S(2)}, u32[]{:S(2)}) async-start(f32[1,16,4096]{2,0,1:T(1,128)} %reshape.440), calls=%async_computation | async-start | bytes 524288 | tf_op jit(solution)/shard_map/all_to_all | solution.py:69
  25.7 11.3 %all-to-all-start.1 = ((f32[1,16,4096]{2,0,1:T(1,128)}), f32[1,16,4096]{2,0,1:T(1,128)S(1)}, u32[]{:S(2)}, u32[]{:S(2)}) async-start(f32[1,16,4096]{2,0,1:T(1,128)} %copy.46), calls=%async_computation.1 | async-start | bytes 524288 | tf_op jit(solution)/shard_map/all_to_all | solution.py:89
  37.0 11.4 %all-to-all-start.2 = ((f32[1,16,4096]{2,0,1:T(1,128)}), f32[1,16,4096]{2,0,1:T(1,128)S(1)}, u32[]{:S(2)}, u32[]{:S(2)}) async-start(f32[1,16,4096]{2,0,1:T(1,128)} %copy.47), calls=%async_computation.2 | async-start | bytes 524288 | tf_op jit(solution)/shard_map/all_to_all | solution.py:90
  66.9 11.0 %copy-start.4 = (f32[1,2048,64]{2,1,0:T(8,128)S(1)}, f32[1,2048,64]{2,1,0:T(8,128)}, u32[]{:S(2)}) copy-start(f32[1,2048,64]{2,1,0:T(8,128)} %get-tuple-element.464) | copy-start | bytes 1572868 | tf_op jit(solution)/shard_map/while
  92.3 11.0 %copy-start.4 = (f32[1,2048,64]{2,1,0:T(8,128)S(1)}, f32[1,2048,64]{2,1,0:T(8,128)}, u32[]{:S(2)}) copy-start(f32[1,2048,64]{2,1,0:T(8,128)} %get-tuple-element.464) | copy-start | bytes 1572868 | tf_op jit(solution)/shard_map/while
  117.8 11.0 %copy-start.4 = (f32[1,2048,64]{2,1,0:T(8,128)S(1)}, f32[1,2048,64]{2,1,0:T(8,128)}, u32[]{:S(2)}) copy-start(f32[1,2048,64]{2,1,0:T(8,128)} %get-tuple-element.464) | copy-start | bytes 1572868 | tf_op jit(solution)/shard_map/while
  143.2 11.0 %copy-start.4 = (f32[1,2048,64]{2,1,0:T(8,128)S(1)}, f32[1,2048,64]{2,1,0:T(8,128)}, u32[]{:S(2)}) copy-start(f32[1,2048,64]{2,1,0:T(8,128)} %get-tuple-element.464) | copy-start | bytes 1572868 | tf_op jit(solution)/shard_map/while
  168.6 11.0 %copy-start.4 = (f32[1,2048,64]{2,1,0:T(8,128)S(1)}, f32[1,2048,64]{2,1,0:T(8,128)}, u32[]{:S(2)}) copy-start(f32[1,2048,64]{2,1,0:T(8,128)} %get-tuple-element.464) | copy-start | bytes 1572868 | tf_op jit(solution)/shard_map/while
  194.0 11.0 %copy-start.4 = (f32[1,2048,64]{2,1,0:T(8,128)S(1)}, f32[1,2048,64]{2,1,0:T(8,128)}, u32[]{:S(2)}) copy-start(f32[1,2048,64]{2,1,0:T(8,128)} %get-tuple-element.464) | copy-start | bytes 1572868 | tf_op jit(solution)/shard_map/while
  219.4 11.0 %copy-start.4 = (f32[1,2048,64]{2,1,0:T(8,128)S(1)}, f32[1,2048,64]{2,1,0:T(8,128)}, u32[]{:S(2)}) copy-start(f32[1,2048,64]{2,1,0:T(8,128)} %get-tuple-element.464) | copy-start | bytes 1572868 | tf_op jit(solution)/shard_map/while
  244.9 11.0 %copy-start.4 = (f32[1,2048,64]{2,1,0:T(8,128)S(1)}, f32[1,2048,64]{2,1,0:T(8,128)}, u32[]{:S(2)}) copy-start(f32[1,2048,64]{2,1,0:T(8,128)} %get-tuple-element.464) | copy-start | bytes 1572868 | tf_op jit(solution)/shard_map/while
  269.0 17.3 %copy-start.5 = (s32[1,16]{1,0:T(1,128)S(1)}, s32[1,16]{1,0:T(1,128)}, u32[]{:S(2)}) copy-start(s32[1,16]{1,0:T(1,128)} %param.13) | copy-start | bytes 196
  269.0 17.3 %copy-start.6 = (s32[1,16]{1,0:T(1,128)S(1)}, s32[1,16]{1,0:T(1,128)}, u32[]{:S(2)}) copy-start(s32[1,16]{1,0:T(1,128)} %param.14) | copy-start | bytes 196
  270.8 11.4 %all-to-all-start.3 = ((f32[1,16,128,1,32]{2,4,3,0,1:T(8,128)}), f32[1,16,128,1,32]{2,4,3,0,1:T(8,128)S(1)}, u32[]{:S(2)}, u32[]{:S(2)}) async-start(f32[1,16,128,1,32]{2,4,3,0,1:T(8,128)} %copy.49), calls=%async_computation.3 | async-start | bytes 524288 | tf_op jit(solution)/shard_map/all_to_all | solution.py:117
  282.2 11.4 %all-to-all-start.4 = ((f32[1,16,128,1,32]{2,4,3,0,1:T(8,128)}), f32[1,16,128,1,32]{2,4,3,0,1:T(8,128)S(1)}, u32[]{:S(2)}, u32[]{:S(2)}) async-start(f32[1,16,128,1,32]{2,4,3,0,1:T(8,128)} %copy.51), calls=%async_computation.4 | async-start | bytes 524288 | tf_op jit(solution)/shard_map/all_to_all | solution.py:124
  286.3 187.0 %reduce-scatter.5.cloned.1.call-start = ((), (), s32[]{:S(2)}) async-start(), calls=%async_computation.8 | async-start | bytes 589824 | tf_op jit(solution)/shard_map/reduce_scatter | solution.py:187
  294.2 14.3 %collective-permute-start = (bf16[1,2048,32]{2,1,0:T(8,128)(2,1)S(1)}, bf16[1,2048,32]{2,1,0:T(8,128)(2,1)S(1)}, u32[]{:S(2)}, u32[]{:S(2)}) collective-permute-start(bf16[1,2048,32]{2,1,0:T(8,128)(2,1)S(1)} %bitcast_select_fusion), channel_id=1, source_target_pairs={{0,128},{128,0},{1,129},{129,1},{2,130},{130,2},{3,131},{131,3},{4... | collective-permute-start | bytes 393224 | tf_op jit(solution)/shard_map/ppermute | solution.py:20
  309.2 5.7 collective-permute-start.1
  312.9 4.9 collective-permute-start.2
  326.0 102.3 %copy-start.7 = (s32[8]{0:T(128)S(1)}, s32[8]{0:T(128)}, u32[]{:S(2)}) copy-start(s32[8]{0:T(128)} %param.15) | copy-start | bytes 100
  326.1 5.6 copy-start.2
  335.8 1.8 copy-start.1
  337.6 2.6 copy-start.3
  340.3 5.6 copy-start.2
  350.0 1.8 copy-start.1
  351.8 2.6 copy-start.3
  354.4 5.6 copy-start.2
  364.2 1.8 copy-start.1
  365.9 2.6 copy-start.3
  368.6 5.6 copy-start.2
  378.3 1.8 copy-start.1
  380.1 2.6 copy-start.3
  424.4 4.0 collective-permute-start.3
  432.8 614.0 %reduce-scatter.3.cloned.1.call-start = ((), (), s32[]{:S(2)}) async-start(), calls=%async_computation.7 | async-start | bytes 2113536 | tf_op jit(solution)/shard_map/reduce_scatter | solution.py:208
Sparse Core Ops, SparseCore 0:
  433.0 40.2 reduce-scatter.4
  476.3 570.4 reduce-scatter.2
where the time goes:
time: 1070 us; the launch traced here: 1060 us
  waiting for transfers between devices  629 us (59%)
  matrix products  202 us (19%)
  local copies, waits for them, and re-layouts  74.6 us (7%)
  blocking collectives  40.1 us (4%)
  starting transfers between devices  34.2 us (3%)
  loops' own time  32.3 us (3%)
  other arithmetic  24.3 us (2%)
  between operations  19.1 us (2%)
    reduce_scatter x1, waiting for transfers between devices, body(): lax.psum_scatter(result, ('grp', 'seq'), scatter_dimension=0, tiled=True)  574 us
    dot_general x8, matrix products, fourier_block(): jnp.einsum('jm,smc->sjc', jnp.sin(angles), stacked, precision=highest)  87.7 us
    dot_general x8, matrix products, fourier_block(): jnp.einsum('jm,smc->sjc', jnp.cos(angles), stacked, precision=highest)  76.7 us
    dynamic_update_slice x32, local copies, waits for them, and re-layouts, body(): lax.map(fourier_block, jnp.arange(length // out_block, dtype=jnp.int32))  28.5 us
    psum x1, blocking collectives, body(): pooled = lax.psum(local_sum, 'seq') / full_len  24.7 us
  transfers between devices with their start and end apart: 11, of which 10 were waited for; matrix products, arithmetic and copies ran while one was open for 2% of the time, Pallas kernels for 0%

commit v1 on v0

v1 whole, which is shorter than its diff:
```python
import functools
import math

import jax
import jax.numpy as jnp
import numpy as np
from jax import lax
from jax.experimental import pallas as pl
from jax.experimental.pallas import tpu as pltpu
from jax.sharding import PartitionSpec as P

MESH = pl.DeviceIdType.MESH
F32 = jnp.float32
BF16 = jnp.bfloat16
HIGHEST = lax.Precision.HIGHEST

C = 64
H = 1024
E = 128
K = 8
SEQLEN = 32768
NSEQ = 16
NGRP = 8
NPAIR = 2
OWN = 2
SPAN = SEQLEN // NSEQ
PAIRS = SPAN // 2
BLOCKS = SPAN // 256
TAU = 0.2
LOSS_SCALE = 256.0
GELU_A = math.sqrt(2.0 / math.pi)
GELU_B = 0.044715 * GELU_A
CHIPS = NSEQ // 2
HB = 256


def split(values):
    high = values.astype(np.float32).astype(BF16)
    low = (values - high.astype(np.float64)).astype(np.float32).astype(BF16)
    return high, low


def transform_tables():
    row = np.arange(256)
    a = (row // 16) * 16 + 2 * (row % 8) + (row % 16) // 8
    col = np.arange(256)
    k1 = 2 * (col % 128) + col // 128
    first = 2 * np.pi * ((a[:, None] * k1[None, :]) % 256) / 256
    first = np.concatenate([np.cos(first), -np.sin(first)], axis=1)
    b = np.arange(128)
    turn = 2 * np.pi * (b[:, None] * k1[None, :]) / SEQLEN
    turn = np.concatenate([np.cos(turn), np.sin(turn)], axis=1).astype(np.float32)
    k2 = np.arange(128)
    second = 2 * np.pi * ((k2[:, None] * b[None, :]) % 128) / 128
    cos, sin = np.cos(second), np.sin(second)
    second = np.block([[cos, sin], [-sin, cos]])
    pick = np.zeros((2, 128, 256), np.float32)
    for odd_row in range(2):
        for step in range(128):
            pick[odd_row, step, 128 * (step % 2) + 64 * odd_row + step // 2] = 1.0
    return (*split(first), turn, *split(second), pick.astype(BF16))


def dot3(a, b_high, b_low, a_low=None):
    dot = functools.partial(jnp.dot, preferred_element_type=F32)
    return dot(a, b_high) + (dot(a, b_low) + dot(a_low, b_high))


def views_kernel(
    send, first_h, first_l, turn, second_h, second_l, pick,
    feat, halo,
    series, rows, time_main, time_halo, freq_main, freq_halo,
    s1, r1, s2, r2, s3, r3,
):
    me = lax.axis_index("seq")
    branch = lax.axis_index("pair")
    other = 1 - branch

    barrier = pltpu.get_barrier_semaphore()

    def greet(i, _):
        @pl.when(i > 0)
        def _():
            peer = lax.rem(me + i, NSEQ)
            pl.semaphore_signal(barrier, 1, device_id={"seq": peer}, device_id_type=MESH)

        peer = lax.rem(me + i, NSEQ)
        pl.semaphore_signal(barrier, 1, device_id={"pair": other, "seq": peer}, device_id_type=MESH)
        return 0

    lax.fori_loop(0, NSEQ, greet, 0)
    pl.semaphore_wait(barrier, 2 * NSEQ - 1)

    def series_copy(i, dst):
        return pltpu.make_async_remote_copy(
            src_ref=send.at[lax.rem(me + i, NSEQ)], dst_ref=series.at[dst],
            send_sem=s1.at[i], recv_sem=r1.at[i],
            device_id={"seq": lax.rem(me + i, NSEQ)}, device_id_type=MESH)

    def start_series(i, _):
        series_copy(i, me).start()
        return 0

    lax.fori_loop(1, NSEQ, start_series, 0)
    series[me] = send[me]

    def wait_series(i, _):
        series_copy(i, lax.rem(me - i + NSEQ, NSEQ)).wait_recv()
        return 0

    lax.fori_loop(1, NSEQ, wait_series, 0)

    lane = lax.broadcasted_iota(jnp.int32, (NSEQ, 128), 1)

    def pack(values, main, edge):
        parts = [v.reshape(NSEQ, BLOCKS, 256) for v in values]
        block = jnp.concatenate(parts, axis=1).astype(BF16)
        main[:, 0] = block[:, :, :128]
        main[:, 1] = block[:, :, 128:]
        for c in range(OWN):
            for half in range(2):
                columns = slice(128 * half, 128 * (half + 1))
                rows[...] = values[c][:, columns]
                low = rows[pl.ds(0, NSEQ, stride=BLOCKS), :]
                high = rows[pl.ds(BLOCKS - 1, NSEQ, stride=BLOCKS), :]
                before = pltpu.roll(high, 1, 0)
                after = pltpu.roll(low, NSEQ - 1, 0)
                both = jnp.where(lane >= 64, before, after)
                for d in range(NSEQ):
                    edge[d, c:c + 1, columns] = both[d:d + 1]

    def view_copies(view, i, main, edge, slot):
        peer = lax.rem(me + i, NSEQ)
        target = {"pair": view, "seq": peer}
        n = view * NSEQ + i
        return (
            pltpu.make_async_remote_copy(
                src_ref=main.at[peer], dst_ref=feat.at[slot], send_sem=s2.at[n],
                recv_sem=r2.at[branch * NSEQ + i], device_id=target, device_id_type=MESH),
            pltpu.make_async_remote_copy(
                src_ref=edge.at[peer], dst_ref=halo.at[slot], send_sem=s3.at[n],
                recv_sem=r3.at[branch * NSEQ + i], device_id=target, device_id_type=MESH),
        )

    mine = branch * NSEQ + me

    def start_view(view, main, edge):
        def step(i, _):
            @pl.when(jnp.logical_or(i > 0, branch != view))
            def _():
                for copy in view_copies(view, i, main, edge, mine):
                    copy.start()
            return 0

        lax.fori_loop(0, NSEQ, step, 0)

        @pl.when(branch == view)
        def _():
            feat[mine] = main[me]
            halo[mine] = edge[me]

    even = [series[:, c, 0:8, :].reshape(128, 128) for c in range(OWN)]
    odd = [series[:, c, 8:16, :].reshape(128, 128) for c in range(OWN)]
    views = [
        jnp.dot(even[c].astype(BF16), pick[0], preferred_element_type=F32)
        + jnp.dot(odd[c].astype(BF16), pick[1], preferred_element_type=F32)
        for c in range(OWN)
    ]
    pack(views, time_main, time_halo)
    start_view(0, time_main, time_halo)

    turned = []
    for c in range(OWN):
        whole = series[:, c].reshape(256, 128)
        flat = jnp.concatenate([whole[:128].T, whole[128:].T], axis=1)
        high = flat.astype(BF16)
        low = (flat - high.astype(F32)).astype(BF16)
        part = dot3(high, first_h[...], first_l[...], low)
        re, im = part[:, :256], part[:, 256:]
        cos, sin = turn[:, :256], turn[:, 256:]
        turned.append(jnp.concatenate([re * cos + im * sin, im * cos - re * sin], axis=0))
    powers = []
    for c in range(OWN):
        high = turned[c].astype(BF16)
        low = (turned[c] - high.astype(F32)).astype(BF16)
        dot = functools.partial(jnp.dot, preferred_element_type=F32)
        spec = dot(second_h[...], high) + (dot(second_h[...], low) + dot(second_l[...], high))
        re, im = spec[:128], spec[128:]
        powers.append(jnp.sqrt(1.0 + (re * re + im * im) * (1.0 / SEQLEN)))
    pack(powers, freq_main, freq_halo)
    start_view(1, freq_main, freq_halo)

    def wait_view(i, _):
        from_own = branch * NSEQ + lax.rem(me - i + NSEQ, NSEQ)
        from_other = other * NSEQ + lax.rem(me - i + NSEQ, NSEQ)

        def arrivals(source, slot):
            peer = lax.rem(me - i + NSEQ, NSEQ)
            target = {"pair": source, "seq": peer}
            return (
                pltpu.make_async_remote_copy(
                    src_ref=freq_main.at[peer], dst_ref=feat.at[slot], send_sem=s2.at[i],
                    recv_sem=r2.at[source * NSEQ + i], device_id=target, device_id_type=MESH),
                pltpu.make_async_remote_copy(
                    src_ref=freq_halo.at[peer], dst_ref=halo.at[slot], send_sem=s3.at[i],
                    recv_sem=r3.at[source * NSEQ + i], device_id=target, device_id_type=MESH),
            )

        @pl.when(i > 0)
        def _():
            for copy in arrivals(branch, from_own):
                copy.wait_recv()

        for copy in arrivals(other, from_other):
            copy.wait_recv()
        return 0

    lax.fori_loop(0, NSEQ, wait_view, 0)

    def wait_sends(i, _):
        @pl.when(i > 0)
        def _():
            series_copy(i, me).wait_send()

        for view, main, edge in ((0, time_main, time_halo), (1, freq_main, freq_halo)):
            @pl.when(jnp.logical_or(i > 0, branch != view))
            def _():
                for copy in view_copies(view, i, main, edge, mine):
                    copy.wait_send()
        return 0

    lax.fori_loop(0, NSEQ, wait_sends, 0)


def make_views(series):
    send = series[0].T.reshape(NSEQ, OWN, BLOCKS, 2, 128).transpose(0, 1, 3, 2, 4)
    send = send.reshape(NSEQ, OWN, 16, 128)
    vmem = pl.BlockSpec(memory_space=pltpu.VMEM)
    tables = [jnp.asarray(t) for t in transform_tables()]
    sources = NPAIR * NSEQ
    return pl.pallas_call(
        views_kernel,
        out_shape=(
            jax.ShapeDtypeStruct((sources, 2, 16, 128), BF16),
            jax.ShapeDtypeStruct((sources, OWN, 256), F32),
        ),
        in_specs=[vmem] * 7,
        out_specs=(vmem, vmem),
        scratch_shapes=[
            pltpu.VMEM((NSEQ, OWN, 16, 128), F32),
            pltpu.VMEM((128, 128), F32),
            pltpu.VMEM((NSEQ, 2, 16, 128), BF16),
            pltpu.VMEM((NSEQ, OWN, 256), F32),
            pltpu.VMEM((NSEQ, 2, 16, 128), BF16),
            pltpu.VMEM((NSEQ, OWN, 256), F32),
            pltpu.SemaphoreType.DMA((NSEQ,)),
            pltpu.SemaphoreType.DMA((NSEQ,)),
            pltpu.SemaphoreType.DMA((sources,)),
            pltpu.SemaphoreType.DMA((sources,)),
            pltpu.SemaphoreType.DMA((sources,)),
            pltpu.SemaphoreType.DMA((sources,)),
        ],
        compiler_params=pltpu.CompilerParams(collective_id=0, has_side_effects=True),
        name="views",
    )(send, *tables)


ROWS = 128


def encoder_kernel(
    time_blocks, freq_blocks, feat, halo, weight,
    encoded, sums, grads,
    tall, edges, wide, turned, across, patches, patches_t, slopes, total,
):
    @pl.when(pl.program_id(0) == 0)
    def _():
        me = lax.axis_index("seq")
        is_time = lax.axis_index("pair") == 0
        listed = [jnp.where(is_time, time_blocks[0, n], freq_blocks[0, n]) for n in range(16)]

        def keep(q):
            block = me * BLOCKS + q
            hit = listed[0] == block
            for n in range(1, 16):
                hit = jnp.logical_or(hit, listed[n] == block)
            drop = jnp.logical_or(hit, jnp.logical_or(block < 0, block >= NSEQ * BLOCKS))
            return jnp.where(drop, 0.0, 1.0).astype(F32)

        for parity in range(2):
            tall[parity * 512:(parity + 1) * 512, :] = (
                feat[:, parity].astype(F32).reshape(512, 128))
            for source in range(NPAIR * NSEQ):
                edges[parity * C + OWN * source:parity * C + OWN * (source + 1), :] = (
                    halo[source, :, parity * 128:(parity + 1) * 128])
        side = lax.broadcasted_iota(jnp.int32, (128, 128), 1)
        rim = edges[...].astype(BF16).astype(F32) * jnp.where(side >= 64, keep(-1), keep(BLOCKS))
        wide[:, 0:128] = rim
        wide[:, 128 + PAIRS:256 + PAIRS] = rim
        rim_t = rim.T
        turned[0:8, :] = rim_t[120:128]
        turned[8 + PAIRS:16 + PAIRS, :] = rim_t[0:8]
        for q in range(BLOCKS):
            piece = tall[pl.ds(q, 128, stride=BLOCKS), :] * keep(q)
            wide[:, 128 * (q + 1):128 * (q + 2)] = piece
            turned[8 + 128 * q:8 + 128 * (q + 1), :] = piece.T
        across[...] = pltpu.roll(turned[...], 64, 1)
        low = lax.broadcasted_iota(jnp.int32, (ROWS, 128), 1) < 64
        for j in range(K // 2):
            columns = slice(128 * j, 128 * (j + 1))
            for r in range(PAIRS // ROWS):
                at = 8 + j - 2 + ROWS * r
                patches[r, 0:ROWS, columns] = turned[at:at + ROWS, :].astype(BF16)
                patches[r, ROWS:2 * ROWS, columns] = jnp.where(
                    low, across[at:at + ROWS, :], across[at + 1:at + 1 + ROWS, :]).astype(BF16)
        shifted = []
        for d in range(-2, 3):
            whole = wide[...]
            if d != 0:
                whole = pltpu.roll(whole, (-d) % (256 + PAIRS), 1)
            part = whole[:, 128:128 + PAIRS].astype(BF16)
            j = d + 2
            if j < K // 2:
                patches_t[128 * j:128 * (j + 1), 0:PAIRS] = part
                patches_t[128 * j:128 * j + 64, PAIRS:] = part[64:]
            if j > 0:
                patches_t[128 * (j - 1) + 64:128 * j, PAIRS:] = part[:64]

    total[...] = jnp.zeros_like(total)
    weights = weight[0]

    def piece(r, _):
        preact = lax.dot_general(
            patches[r], weights, (((1,), (1,)), ((), ())), preferred_element_type=F32)
        square = preact * preact
        inner = preact * (GELU_A + GELU_B * square)
        gate = 0.5 + 0.5 * jnp.tanh(inner)
        active = preact * gate
        slope = gate + active * ((1.0 - gate) * (2.0 * GELU_A + (6.0 * GELU_B) * square))
        pair = active[:ROWS] + active[ROWS:]
        encoded[0, 0, pl.ds(r * ROWS, ROWS), :] = (pair * 0.5).astype(BF16)
        total[...] += jnp.sum(pair.reshape(ROWS // 8, 8, HB), axis=0)
        slope = slope.astype(BF16)
        slopes[pl.ds(r * ROWS, ROWS), :] = slope[:ROWS]
        slopes[pl.ds(PAIRS + r * ROWS, ROWS), :] = slope[ROWS:]
        return 0

    lax.fori_loop(0, PAIRS // ROWS, piece, 0)
    sums[...] = total[...]
    grad_t = jnp.dot(patches_t[...], slopes[...], preferred_element_type=F32)
    grad = grad_t.T.reshape(2, NSEQ, 8, K * C)
    grads[...] = jnp.concatenate([grad[0], grad[1]], axis=1).reshape(
        CHIPS, 2, 16, K * C)


def encode(time_blocks, freq_blocks, feat, halo, conv_weight):
    smem = pl.BlockSpec(memory_space=pltpu.SMEM)
    sources = NPAIR * NSEQ
    return pl.pallas_call(
        encoder_kernel,
        grid=(H // HB,),
        out_shape=(
            jax.ShapeDtypeStruct((1, 1, PAIRS, H), BF16),
            jax.ShapeDtypeStruct((8, H), F32),
            jax.ShapeDtypeStruct((CHIPS, 2, 8 * NGRP, K * C), F32),
        ),
        in_specs=[
            smem,
            smem,
            pl.BlockSpec((sources, 2, 16, 128), lambda n: (0, 0, 0, 0)),
            pl.BlockSpec((sources, OWN, 256), lambda n: (0, 0, 0)),
            pl.BlockSpec((1, HB, K * C), lambda n: (0, n, 0)),
        ],
        out_specs=(
            pl.BlockSpec((1, 1, PAIRS, HB), lambda n: (0, 0, 0, n)),
            pl.BlockSpec((8, HB), lambda n: (0, n)),
            pl.BlockSpec((CHIPS, 2, 16, K * C), lambda n: (0, 0, n, 0)),
        ),
        scratch_shapes=[
            pltpu.VMEM((8 * 2 * C, 128), F32),
            pltpu.VMEM((2 * C, 128), F32),
            pltpu.VMEM((2 * C, 256 + PAIRS), F32),
            pltpu.VMEM((16 + PAIRS, 128), F32),
            pltpu.VMEM((16 + PAIRS, 128), F32),
            pltpu.VMEM((PAIRS // ROWS, 2 * ROWS, K * C), BF16),
            pltpu.VMEM((K * C, SPAN), BF16),
            pltpu.VMEM((SPAN, HB), BF16),
            pltpu.VMEM((8, HB), F32),
        ],
        compiler_params=pltpu.CompilerParams(vmem_limit_bytes=48 * 1024 * 1024),
        name="encoder",
    )(time_blocks, freq_blocks, feat, halo, conv_weight)


def reduce_kernel(
    positives, sums, grads, proj,
    conv_out, proj_out, loss_out,
    own_sum, all_sums, notes, own_notes, other_notes, own_rows, other_rows, table,
    core_in, passed, chip_in, ready, grp_in,
    s_sum, r_sum, s_own, r_own, s_oth, r_oth, s_core, r_core, s_chip, r_chip, s_grp, r_grp,
):
    me = lax.axis_index("seq")
    branch = lax.axis_index("pair")
    grp = lax.axis_index("grp")
    other = 1 - branch
    chip, core = me // 2, lax.rem(me, 2)
    sibling = me + 1 - 2 * core

    barrier = pltpu.get_barrier_semaphore()

    def greet_seq(i, _):
        pl.semaphore_signal(
            barrier, 1, device_id={"seq": lax.rem(me + i, NSEQ)}, device_id_type=MESH)
        return 0

    def greet_grp(i, _):
        peer = lax.rem(grp + i, NGRP)

        @pl.when(i > 0)
        def _():
            pl.semaphore_signal(barrier, 1, device_id={"grp": peer}, device_id_type=MESH)

        pl.semaphore_signal(
            barrier, 1, device_id={"pair": other, "grp": peer}, device_id_type=MESH)
        return 0

    lax.fori_loop(1, NSEQ, greet_seq, 0)
    lax.fori_loop(0, NGRP, greet_grp, 0)
    own_sum[...] = jnp.sum(sums[...], axis=0, keepdims=True)
    pl.semaphore_wait(barrier, NSEQ - 1 + 2 * NGRP - 1)

    def sum_copy(i, slot):
        return pltpu.make_async_remote_copy(
            src_ref=own_sum, dst_ref=all_sums.at[slot], send_sem=s_sum.at[i],
            recv_sem=r_sum.at[i], device_id={"seq": lax.rem(me + i, NSEQ)}, device_id_type=MESH)

    def start_sum(i, _):
        sum_copy(i, me).start()
        return 0

    lax.fori_loop(1, NSEQ, start_sum, 0)
    all_sums[me] = own_sum[...]

    def core_copy(i):
        j = lax.rem(chip + i, CHIPS)
        return pltpu.make_async_remote_copy(
            src_ref=grads.at[j, 1 - core], dst_ref=core_in.at[j], send_sem=s_core.at[i],
            recv_sem=r_core.at[i], device_id={"seq": sibling}, device_id_type=MESH)

    def chip_copy(i, slot):
        j = lax.rem(chip + i, CHIPS)
        return pltpu.make_async_remote_copy(
            src_ref=passed.at[j], dst_ref=chip_in.at[slot], send_sem=s_chip.at[i],
            recv_sem=r_chip.at[i], device_id={"seq": 2 * j + core}, device_id_type=MESH)

    def start_core(i, _):
        core_copy(lax.rem(i, CHIPS)).start()
        return 0

    lax.fori_loop(1, CHIPS + 1, start_core, 0)
    table[...] = proj[0].astype(F32)

    def pass_on(i, _):
        core_copy(i).wait_recv()
        j = lax.rem(chip + i, CHIPS)
        passed[j] = grads[j, core] + core_in[j]
        chip_copy(i, chip).start()
        return 0

    lax.fori_loop(1, CHIPS, pass_on, 0)

    def wait_sum(i, _):
        sum_copy(i, lax.rem(me - i + NSEQ, NSEQ)).wait_recv()
        return 0

    lax.fori_loop(1, NSEQ, wait_sum, 0)
    pooled = jnp.sum(all_sums[...], axis=0) * (1.0 / SEQLEN)
    latent = jnp.dot(
        jnp.broadcast_to(pooled, (8, H)), table[...], precision=HIGHEST,
        preferred_element_type=F32)[0:1]
    for g in range(NGRP):
        notes[g] = jnp.concatenate([latent, pooled[:, 128 * g:128 * (g + 1)]], axis=1)

    def own_copy(i, slot):
        peer = lax.rem(grp + i, NGRP)
        return pltpu.make_async_remote_copy(
            src_ref=notes.at[peer], dst_ref=own_notes.at[slot], send_sem=s_own.at[i],
            recv_sem=r_own.at[i], device_id={"grp": peer}, device_id_type=MESH)

    def other_copy(i, slot):
        peer = lax.rem(grp + i, NGRP)
        return pltpu.make_async_remote_copy(
            src_ref=notes.at[peer], dst_ref=other_notes.at[slot], send_sem=s_oth.at[i],
            recv_sem=r_oth.at[i], device_id={"pair": other, "grp": peer}, device_id_type=MESH)

    def start_notes(i, _):
        @pl.when(i > 0)
        def _():
            own_copy(i, grp).start()

        other_copy(i, grp).start()
        return 0

    lax.fori_loop(0, NGRP, start_notes, 0)
    own_notes[grp] = notes[grp]

    def wait_notes(i, _):
        source = lax.rem(grp - i + NGRP, NGRP)

        @pl.when(i > 0)
        def _():
            own_copy(i, source).wait_recv()

        other_copy(i, source).wait_recv()
        return 0

    lax.fori_loop(0, NGRP, wait_notes, 0)
    for g in range(NGRP):
        own_rows[g:g + 1, :] = own_notes[g]
        other_rows[g:g + 1, :] = other_notes[g]
    z_own, z_other = own_rows[:, :E], other_rows[:, :E]
    r_own_ = lax.rsqrt(jnp.sum(z_own * z_own, axis=1, keepdims=True) + 1e-06)
    r_other_ = lax.rsqrt(jnp.sum(z_other * z_other, axis=1, keepdims=True) + 1e-06)
    e_own, e_other = z_own * r_own_, z_other * r_other_
    is_time = branch == 0
    time_emb = jnp.where(is_time, e_own, e_other)
    freq_emb = jnp.where(is_time, e_other, e_own)
    dot = functools.partial(
        lax.dot_general, precision=HIGHEST, preferred_element_type=F32)
    logits = dot(time_emb, freq_emb, (((1,), (1,)), ((), ()))) * (1.0 / TAU)
    row = lax.broadcasted_iota(jnp.int32, (NGRP, NGRP), 0)
    col = lax.broadcasted_iota(jnp.int32, (NGRP, NGRP), 1)
    target = jnp.zeros((NGRP, NGRP), F32)
    for i in range(NGRP):
        target = jnp.where(jnp.logical_and(row == i, col == positives[i]), 1.0, target)
    exponent = jnp.exp(logits)
    by_row = jnp.sum(exponent, axis=1, keepdims=True)
    by_col = jnp.sum(exponent, axis=0, keepdims=True)
    picked = jnp.sum(jnp.sum(target * logits, axis=1, keepdims=True), axis=0, keepdims=True)
    lse = jnp.sum(jnp.log(by_row), axis=0, keepdims=True) + jnp.sum(
        jnp.log(by_col), axis=1, keepdims=True)
    loss_out[...] = (lse - 2.0 * picked) * (1.0 / (2 * NGRP))
    slope = (exponent / by_row + exponent / by_col - 2.0 * target) * (
        LOSS_SCALE / (TAU * 2 * NGRP))
    d_time = dot(slope, freq_emb, (((1,), (0,)), ((), ())))
    d_freq = dot(slope, time_emb, (((0,), (0,)), ((), ())))
    d_emb = jnp.where(is_time, d_time, d_freq)
    inner = jnp.sum(z_own * d_emb, axis=1, keepdims=True)
    d_latent = r_own_ * d_emb - z_own * (r_own_ * r_own_ * r_own_ * inner)
    proj_out[0] = dot(own_rows[:, E:], d_latent, (((0,), (0,)), ((), ())))
    sample = lax.broadcasted_iota(jnp.int32, (NGRP, E), 0)
    d_mine = jnp.sum(jnp.where(sample == grp, d_latent, 0.0), axis=0, keepdims=True)

    core_copy(0).wait_recv()
    whole = grads[chip, core] + core_in[chip]

    def wait_chip(i, _):
        chip_copy(i, lax.rem(chip - i + CHIPS, CHIPS)).wait_recv()
        return 0

    lax.fori_loop(1, CHIPS, wait_chip, 0)
    chip_in[chip] = jnp.zeros((8 * NGRP, K * C), F32)
    for j in range(CHIPS):
        whole = whole + chip_in[j]
    for g in range(NGRP):
        at = pl.multiple_of(128 * g + 8 * me, 8)
        factor = jnp.sum(table[pl.ds(at, 8), :] * d_mine, axis=1, keepdims=True)
        ready[g] = whole[8 * g:8 * (g + 1)] * (factor * (1.0 / SEQLEN))

    def grp_copy(i, slot):
        peer = lax.rem(grp + i, NGRP)
        return pltpu.make_async_remote_copy(
            src_ref=ready.at[peer], dst_ref=grp_in.at[slot], send_sem=s_grp.at[i],
            recv_sem=r_grp.at[i], device_id={"grp": peer}, device_id_type=MESH)

    def start_grp(i, _):
        grp_copy(i, grp).start()
        return 0

    lax.fori_loop(1, NGRP, start_grp, 0)
    grp_in[grp] = ready[grp]

    def wait_grp(i, _):
        grp_copy(i, lax.rem(grp - i + NGRP, NGRP)).wait_recv()
        return 0

    lax.fori_loop(1, NGRP, wait_grp, 0)
    result = grp_in[0]
    for g in range(1, NGRP):
        result = result + grp_in[g]
    conv_out[0] = result

    def sent_seq(i, _):
        sum_copy(i, me).wait_send()
        return 0

    def sent_chip(i, _):
        core_copy(i).wait_send()

        @pl.when(i > 0)
        def _():
            chip_copy(i, chip).wait_send()
            own_copy(i, grp).wait_send()
            grp_copy(i, grp).wait_send()

        other_copy(i, grp).wait_send()
        return 0

    lax.fori_loop(1, NSEQ, sent_seq, 0)
    lax.fori_loop(0, CHIPS, sent_chip, 0)


def reduce_all(positives, sums, grads, proj_weight):
    vmem = pl.BlockSpec(memory_space=pltpu.VMEM)
    smem = pl.BlockSpec(memory_space=pltpu.SMEM)
    part = (8 * NGRP, K * C)
    dma = pltpu.SemaphoreType.DMA
    return pl.pallas_call(
        reduce_kernel,
        out_shape=(
            jax.ShapeDtypeStruct((1, 8, K * C), F32),
            jax.ShapeDtypeStruct((1, H // NGRP, E), F32),
            jax.ShapeDtypeStruct((1, 1), F32),
        ),
        in_specs=[smem, vmem, vmem, vmem],
        out_specs=(vmem, vmem, vmem),
        scratch_shapes=[
            pltpu.VMEM((1, H), F32),
            pltpu.VMEM((NSEQ, 1, H), F32),
            pltpu.VMEM((NGRP, 1, 2 * E), F32),
            pltpu.VMEM((NGRP, 1, 2 * E), F32),
            pltpu.VMEM((NGRP, 1, 2 * E), F32),
            pltpu.VMEM((NGRP, 2 * E), F32),
            pltpu.VMEM((NGRP, 2 * E), F32),
            pltpu.VMEM((H, E), F32),
            pltpu.VMEM((CHIPS, *part), F32),
            pltpu.VMEM((CHIPS, *part), F32),
            pltpu.VMEM((CHIPS, *part), F32),
            pltpu.VMEM((NGRP, 8, K * C), F32),
            pltpu.VMEM((NGRP, 8, K * C), F32),
            dma((NSEQ,)), dma((NSEQ,)),
            dma((NGRP,)), dma((NGRP,)),
            dma((NGRP,)), dma((NGRP,)),
            dma((CHIPS,)), dma((CHIPS,)),
            dma((CHIPS,)), dma((CHIPS,)),
            dma((NGRP,)), dma((NGRP,)),
        ],
        compiler_params=pltpu.CompilerParams(collective_id=1, has_side_effects=True),
        name="reduce",
    )(positives, sums, grads, proj_weight)


def body(series, time_blocks, freq_blocks, positives, conv_weight, proj_weight):
    feat, halo = make_views(series)
    encoded, sums, grads = encode(time_blocks, freq_blocks, feat, halo, conv_weight)
    conv_share, proj_share, loss = reduce_all(positives, sums, grads, proj_weight)
    return (encoded, loss[0, 0], conv_share, proj_share)


def solution(mesh):
    in_specs = (
        P("grp", "seq", "pair"),
        P("grp", None),
        P("grp", None),
        P(),
        P("pair", None, None),
        P("pair", None, None),
    )
    out_specs = (
        P("pair", "grp", "seq", None),
        P(),
        P("pair", ("grp", "seq"), None),
        P("pair", "grp", None),
    )
    return jax.shard_map(body, mesh=mesh, in_specs=in_specs, out_specs=out_specs, check_vma=False)
```

time: 1070 us -> 86.5 us (0.08); the launches traced: 1060 us -> 86.1 us
  waiting for transfers between devices: 629 us -> 0 us
  matrix products: 202 us -> 0 us
  Pallas kernels: 0 us -> 75.2 us
  local copies, waits for them, and re-layouts: 74.6 us -> 8.51 us
  blocking collectives: 40.1 us -> 0 us
  starting transfers between devices: 34.2 us -> 0 us
  loops' own time: 32.3 us -> 0 us
  other arithmetic: 24.3 us -> 0 us
  between operations: 19.1 us -> 2.46 us
    reduce_scatter x2 -> x0, waiting for transfers between devices: 582 us -> none  [the longest x1 574 us: body(): lax.psum_scatter(result, ('grp', 'seq'), scatter_dimension=0, tiled=True)]
    dot_general x31 -> x0, matrix products: 202 us -> none  [the longest x8 87.7 us: fourier_block(): jnp.einsum('jm,smc->sjc', jnp.sin(angles), stacked, precision=highest)]
    pallas_call x0 -> x3, Pallas kernels: none -> 75.2 us  [the longest x1 35.9 us: reduce_all(): pl.pallas_call(reduce_kernel, out_shape=(jax.ShapeDtypeStruct((1, 8, K *...]
    another operation x3 -> x0, loops' own time: 32.3 us -> none  [the longest x1 18.9 us: body(): lax.map(fourier_block, jnp.arange(length // out_block, dtype=jnp.int32))]
    all_to_all x5 -> x0, waiting for transfers between devices: 30.6 us -> none  [the longest x1 7.03 us: body(): lax.all_to_all(spec_im.reshape(samples, groups, block_len, 1, own_chan),...]
    dynamic_update_slice x36 -> x0, local copies, waits for them, and re-layouts: 28.7 us -> none  [the longest x32 28.5 us: body(): lax.map(fourier_block, jnp.arange(length // out_block, dtype=jnp.int32))]
    psum x1 -> x0, blocking collectives: 24.7 us -> none  [body(): pooled = lax.psum(local_sum, 'seq') / full_len]
    all_to_all x5 -> x0, starting transfers between devices: 23.1 us -> none  [the longest x1 6.82 us: body(): lax.all_to_all(flat_in, 'seq', split_axis=1, concat_axis=1, tiled=True)]
  transfers between devices with their start and end apart: 11 -> 0, of which waited for: 10 -> 0; matrix products, arithmetic and copies ran while one was open for 2% -> 0% of each run, Pallas kernels for 0% -> 0%
where the time goes in v1:
time: 86.5 us; the launch traced here: 86.1 us
  Pallas kernels  75.2 us (87%)
  local copies, waits for them, and re-layouts  8.51 us (10%)
  between operations  2.46 us (3%)
    pallas_call x1, Pallas kernels, reduce_all(): pl.pallas_call(reduce_kernel, out_shape=(jax.ShapeDtypeStruct((1, 8, K *...  35.9 us
    pallas_call x1, Pallas kernels, make_views(): pl.pallas_call(views_kernel, out_shape=(jax.ShapeDtypeStruct((sources, 2,...  22.5 us
    pallas_call x1, Pallas kernels, encode(): pl.pallas_call(encoder_kernel, grid=(H // HB,), out_shape=(jax.ShapeDtype...  16.8 us
    unnamed x16, local copies, waits for them, and re-layouts  6.54 us
    reshape x2, local copies, waits for them, and re-layouts, make_views(): series[0].T.reshape(NSEQ, OWN, BLOCKS, 2, 128).transpose(0, 1, 3, 2, 4)  1.98 us

profile of v1, /device:TPU:1, one launch (start us, length us, event | category | flops | bytes accessed | tf_op | source)
XLA Modules:
  0.0 86.1 jit_solution(9127347820235780457)
XLA Ops:
  0.6 0.0 copy-start.1
  0.6 0.0 copy-start.6
  0.7 0.0 copy-start.5
  0.7 1.3 %reshape.14 = f32[16,2,8,2,128]{4,3,2,1,0:T(2,128)S(1)} reshape(f32[32,2048]{1,0:T(8,128)} %bitcast.10) | data formatting | bytes 524288 | tf_op jit(solution)/shard_map/reshape | solution.py:236
  1.9 0.7 copy.18
  2.6 22.5 %views.1 = (bf16[32,2,16,128]{3,2,1,0:T(8,128)(2,1)}, f32[32,2,256]{2,1,0:T(2,128)}) custom-call(f32[16,2,16,128]{3,2,1,0:T(8,128)} %bitcast.9, bf16[256,512]{1,0:T(8,128)(2,1)} %constant.12.clone.first_h, bf16[256,512]{1,0:T(8,128)(2,1)} %constant.13.clone.first_l, f32[128,512]{1,0:T(8,128)} %constant.14.clone.turn, ...), custom_call_target="tpu_custom_call" | custom-call | tf_op jit(solution)/shard_map/views/pallas_call | solution.py:241
  25.1 0.0 copy-done.1
  25.1 0.0 copy-done.6
  25.1 0.0 copy-done.5
  25.1 0.0 copy-start.2
  25.1 0.9 %copy-done.2 = bf16[32,2,16,128]{3,2,1,0:T(8,128)(2,1)S(1)} copy-done((bf16[32,2,16,128]{3,2,1,0:T(8,128)(2,1)S(1)}, bf16[32,2,16,128]{3,2,1,0:T(8,128)(2,1)}, u32[]{:S(2)}) %copy-start.2) | copy-done | bytes 262168
  26.1 0.0 copy-start.3
  26.1 0.8 copy-done.3
  26.9 16.8 %encoder.1 = (bf16[1,1,1024,1024]{3,2,1,0:T(8,128)(2,1)}, f32[8,1024]{1,0:T(8,128)S(1)}, f32[8,2,64,512]{3,2,1,0:T(8,128)S(1)}) custom-call(s32[1,16]{1,0:T(1,128)S(1)} %copy-done.5, s32[1,16]{1,0:T(1,128)S(1)} %copy-done.6, bf16[32,2,16,128]{3,2,1,0:T(8,128)(2,1)S(1)} %copy-done.2, f32[32,2,256]{2,1,0:T(2,128)S(1)} %copy-done.3, ...), custom_call_target="tpu_custom_call" | custom-call | tf_op jit(solution)/shard_map/encoder/pallas_call | solution.py:359
  43.8 0.0 copy-start
  43.8 1.3 %copy-done = f32[8,2,64,512]{3,2,1,0:T(8,128)} copy-done((f32[8,2,64,512]{3,2,1,0:T(8,128)}, f32[8,2,64,512]{3,2,1,0:T(8,128)S(1)}, u32[]{:S(2)}) %copy-start) | copy-done | bytes 2097176
  45.1 0.0 copy-start.4
  45.1 0.6 copy-done.4
  45.7 35.9 %reduce.1 = (f32[1,8,512]{2,1,0:T(8,128)}, f32[1,128,128]{2,1,0:T(8,128)}, f32[1,1]{1,0:T(1,128)}) custom-call(s32[8]{0:T(128)} %positives.1, f32[8,1024]{1,0:T(8,128)} %copy-done.4, f32[8,2,64,512]{3,2,1,0:T(8,128)} %copy-done, bf16[1,1024,128]{2,1,0:T(8,128)(2,1)} %proj.1), custom_call_target="tpu_custom_call" | custom-call | tf_op jit(solution)/shard_map/reduce/pallas_call | solution.py:618
  82.2 1.3 %copy.23 = f32[1,8,512]{2,1,0:T(8,128)} copy(f32[1,8,512]{2,1,0:T(8,128)} %get-tuple-element.26) | data formatting | bytes 32768
  83.5 1.5 %copy.24 = f32[1,128,128]{2,1,0:T(8,128)} copy(f32[1,128,128]{2,1,0:T(8,128)} %get-tuple-element.27) | data formatting | bytes 131072
Async XLA Ops:
  0.6 24.5 %copy-start.1 = (bf16[1,1024,512]{2,1,0:T(8,128)(2,1)S(1)}, bf16[1,1024,512]{2,1,0:T(8,128)(2,1)}, u32[]{:S(2)}) copy-start(bf16[1,1024,512]{2,1,0:T(8,128)(2,1)} %weight.1) | copy-start | bytes 3145732
  0.6 24.5 %copy-start.6 = (s32[1,16]{1,0:T(1,128)S(1)}, s32[1,16]{1,0:T(1,128)}, u32[]{:S(2)}) copy-start(s32[1,16]{1,0:T(1,128)} %freq_blocks.1) | copy-start | bytes 196
  0.7 24.5 %copy-start.5 = (s32[1,16]{1,0:T(1,128)S(1)}, s32[1,16]{1,0:T(1,128)}, u32[]{:S(2)}) copy-start(s32[1,16]{1,0:T(1,128)} %time_blocks.1) | copy-start | bytes 196
  25.1 1.0 %copy-start.2 = (bf16[32,2,16,128]{3,2,1,0:T(8,128)(2,1)S(1)}, bf16[32,2,16,128]{3,2,1,0:T(8,128)(2,1)}, u32[]{:S(2)}) copy-start(bf16[32,2,16,128]{3,2,1,0:T(8,128)(2,1)} %get-tuple-element.12.feat) | copy-start | bytes 786436
  26.1 0.8 copy-start.3
  43.8 1.3 %copy-start = (f32[8,2,64,512]{3,2,1,0:T(8,128)}, f32[8,2,64,512]{3,2,1,0:T(8,128)S(1)}, u32[]{:S(2)}) copy-start(f32[8,2,64,512]{3,2,1,0:T(8,128)S(1)} %get-tuple-element.16.grads) | copy-start | bytes 6291460
  45.1 0.6 copy-start.4

commit v2 on v1

v2 whole, which is shorter than its diff:
```python
import functools
import math

import jax
import jax.numpy as jnp
import numpy as np
from jax import lax
from jax.experimental import pallas as pl
from jax.experimental.pallas import tpu as pltpu
from jax.sharding import PartitionSpec as P

MESH = pl.DeviceIdType.MESH
F32 = jnp.float32
BF16 = jnp.bfloat16
HIGHEST = lax.Precision.HIGHEST

C = 64
H = 1024
E = 128
K = 8
SEQLEN = 32768
NSEQ = 16
NGRP = 8
NPAIR = 2
OWN = 2
SPAN = SEQLEN // NSEQ
PAIRS = SPAN // 2
BLOCKS = SPAN // 256
TAU = 0.2
LOSS_SCALE = 256.0
GELU_A = math.sqrt(2.0 / math.pi)
GELU_B = 0.044715 * GELU_A
CHIPS = NSEQ // 2
HB = 256
BANDS = H // HB
ROWS = 128
PIECES = PAIRS // ROWS
DEPTH = 2


def split(values):
    high = values.astype(np.float32).astype(BF16)
    low = (values - high.astype(np.float64)).astype(np.float32).astype(BF16)
    return high, low


def transform_tables():
    row = np.arange(256)
    a = (row // 16) * 16 + 2 * (row % 8) + (row % 16) // 8
    col = np.arange(256)
    k1 = 2 * (col % 128) + col // 128
    first = 2 * np.pi * ((a[:, None] * k1[None, :]) % 256) / 256
    first = np.concatenate([np.cos(first), -np.sin(first)], axis=1)
    b = np.arange(128)
    turn = 2 * np.pi * (b[:, None] * k1[None, :]) / SEQLEN
    turn = np.concatenate([np.cos(turn), np.sin(turn)], axis=1).astype(np.float32)
    k2 = np.arange(128)
    second = 2 * np.pi * ((k2[:, None] * b[None, :]) % 128) / 128
    cos, sin = np.cos(second), np.sin(second)
    second = np.block([[cos, sin], [-sin, cos]])
    pick = np.zeros((2, 128, 256), np.float32)
    for odd_row in range(2):
        for step in range(128):
            pick[odd_row, step, 128 * (step % 2) + 64 * odd_row + step // 2] = 1.0
    return (*split(first), turn, *split(second), pick.astype(BF16))


def dot3(a, b_high, b_low, a_low=None):
    dot = functools.partial(jnp.dot, preferred_element_type=F32)
    return dot(a, b_high) + (dot(a, b_low) + dot(a_low, b_high))


def step_kernel(
    positives, time_blocks, freq_blocks, series_in, weight_in, proj_in,
    first_h_in, first_l_in, turn_in, second_h_in, second_l_in, pick_in,
    encoded, conv_out, proj_out, loss_out,
    raw, weight, proj, first_h, first_l, turn, second_h, second_l, pick,
    send, series, rows, time_main, time_halo, freq_main, freq_halo, feat, halo,
    tall, edges, wide, turned, across, patches, patches_t, held, total, grad_t,
    own_sum, all_sums, notes, own_notes, other_notes, own_rows, other_rows, table,
    grads, core_in, passed, chip_in, ready, grp_in,
    s_in, s_enc, s1, r1, s2, r2, s3, r3,
    s_sum, r_sum, s_own, r_own, s_oth, r_oth, s_core, r_core, s_chip, r_chip, s_grp, r_grp,
):
    me = lax.axis_index("seq")
    branch = lax.axis_index("pair")
    grp = lax.axis_index("grp")
    other = 1 - branch
    chip, core = me // 2, lax.rem(me, 2)
    sibling = me + 1 - 2 * core
    is_time = branch == 0

    loads = [
        pltpu.make_async_copy(src, dst, s_in.at[n])
        for n, (src, dst) in enumerate((
            (series_in, raw), (pick_in, pick), (first_h_in, first_h), (first_l_in, first_l),
            (turn_in, turn), (second_h_in, second_h), (second_l_in, second_l),
            (weight_in, weight), (proj_in, proj)))
    ]
    for load in loads:
        load.start()

    barrier = pltpu.get_barrier_semaphore()

    def greet_seq(i, _):
        peer = lax.rem(me + i, NSEQ)

        @pl.when(i > 0)
        def _():
            pl.semaphore_signal(barrier, 1, device_id={"seq": peer}, device_id_type=MESH)

        pl.semaphore_signal(barrier, 1, device_id={"pair": other, "seq": peer}, device_id_type=MESH)
        return 0

    def greet_grp(i, _):
        peer = lax.rem(grp + i, NGRP)
        pl.semaphore_signal(barrier, 1, device_id={"grp": peer}, device_id_type=MESH)
        pl.semaphore_signal(barrier, 1, device_id={"pair": other, "grp": peer}, device_id_type=MESH)
        return 0

    lax.fori_loop(0, NSEQ, greet_seq, 0)
    lax.fori_loop(1, NGRP, greet_grp, 0)

    loads[0].wait()
    for q in range(BLOCKS):
        for odd in range(2):
            at = 128 * (2 * q + odd)
            send[pl.ds(8 * odd + q, NSEQ * OWN, stride=16), :] = raw[:, at:at + 128]
    pl.semaphore_wait(barrier, 2 * NSEQ - 1 + 2 * (NGRP - 1))

    def series_copy(i, dst):
        peer = lax.rem(me + i, NSEQ)
        return pltpu.make_async_remote_copy(
            src_ref=send.at[pl.ds(pl.multiple_of(32 * peer, 32), 32)], dst_ref=series.at[dst],
            send_sem=s1.at[i], recv_sem=r1.at[i], device_id={"seq": peer}, device_id_type=MESH)

    def start_series(i, _):
        series_copy(i, me).start()
        return 0

    lax.fori_loop(1, NSEQ, start_series, 0)
    series[me] = send[pl.ds(pl.multiple_of(32 * me, 32), 32), :]
    for load in loads[1:]:
        load.wait()
    table[...] = proj[0].astype(F32)

    def wait_series(i, _):
        series_copy(i, lax.rem(me - i + NSEQ, NSEQ)).wait_recv()
        return 0

    lax.fori_loop(1, NSEQ, wait_series, 0)

    lane = lax.broadcasted_iota(jnp.int32, (NSEQ, 128), 1)

    def pack(values, main, edge):
        parts = [v.reshape(NSEQ, BLOCKS, 256) for v in values]
        block = jnp.concatenate(parts, axis=1).astype(BF16)
        main[:, 0] = block[:, :, :128]
        main[:, 1] = block[:, :, 128:]
        for c in range(OWN):
            for half in range(2):
                columns = slice(128 * half, 128 * (half + 1))
                rows[...] = values[c][:, columns]
                low = rows[pl.ds(0, NSEQ, stride=BLOCKS), :]
                high = rows[pl.ds(BLOCKS - 1, NSEQ, stride=BLOCKS), :]
                before = pltpu.roll(high, 1, 0)
                after = pltpu.roll(low, NSEQ - 1, 0)
                both = jnp.where(lane >= 64, before, after)
                for d in range(NSEQ):
                    edge[d, c:c + 1, columns] = both[d:d + 1]

    def view_copies(view, i, main, edge, slot):
        peer = lax.rem(me + i, NSEQ)
        target = {"pair": view, "seq": peer}
        n = view * NSEQ + i
        return (
            pltpu.make_async_remote_copy(
                src_ref=main.at[peer], dst_ref=feat.at[slot], send_sem=s2.at[n],
                recv_sem=r2.at[branch * NSEQ + i], device_id=target, device_id_type=MESH),
            pltpu.make_async_remote_copy(
                src_ref=edge.at[peer], dst_ref=halo.at[slot], send_sem=s3.at[n],
                recv_sem=r3.at[branch * NSEQ + i], device_id=target, device_id_type=MESH),
        )

    mine = branch * NSEQ + me

    def start_view(view, main, edge):
        def step(i, _):
            @pl.when(jnp.logical_or(i > 0, branch != view))
            def _():
                for copy in view_copies(view, i, main, edge, mine):
                    copy.start()
            return 0

        lax.fori_loop(0, NSEQ, step, 0)

        @pl.when(branch == view)
        def _():
            feat[mine] = main[me]
            halo[mine] = edge[me]

    even = [series[:, 16 * c:16 * c + 8, :].reshape(128, 128) for c in range(OWN)]
    odd = [series[:, 16 * c + 8:16 * c + 16, :].reshape(128, 128) for c in range(OWN)]
    views = [
        jnp.dot(even[c].astype(BF16), pick[0], preferred_element_type=F32)
        + jnp.dot(odd[c].astype(BF16), pick[1], preferred_element_type=F32)
        for c in range(OWN)
    ]
    pack(views, time_main, time_halo)
    start_view(0, time_main, time_halo)

    spun = []
    for c in range(OWN):
        whole = series[:, 16 * c:16 * c + 16, :].reshape(256, 128)
        flat = jnp.concatenate([whole[:128].T, whole[128:].T], axis=1)
        high = flat.astype(BF16)
        low = (flat - high.astype(F32)).astype(BF16)
        part = dot3(high, first_h[...], first_l[...], low)
        re, im = part[:, :256], part[:, 256:]
        cos, sin = turn[:, :256], turn[:, 256:]
        spun.append(jnp.concatenate([re * cos + im * sin, im * cos - re * sin], axis=0))
    powers = []
    for c in range(OWN):
        high = spun[c].astype(BF16)
        low = (spun[c] - high.astype(F32)).astype(BF16)
        dot = functools.partial(jnp.dot, preferred_element_type=F32)
        spec = dot(second_h[...], high) + (dot(second_h[...], low) + dot(second_l[...], high))
        re, im = spec[:128], spec[128:]
        powers.append(jnp.sqrt(1.0 + (re * re + im * im) * (1.0 / SEQLEN)))
    pack(powers, freq_main, freq_halo)
    start_view(1, freq_main, freq_halo)

    def wait_view(i, _):
        peer = lax.rem(me - i + NSEQ, NSEQ)

        def arrivals(source):
            slot = source * NSEQ + peer
            target = {"pair": source, "seq": peer}
            return (
                pltpu.make_async_remote_copy(
                    src_ref=freq_main.at[peer], dst_ref=feat.at[slot], send_sem=s2.at[i],
                    recv_sem=r2.at[source * NSEQ + i], device_id=target, device_id_type=MESH),
                pltpu.make_async_remote_copy(
                    src_ref=freq_halo.at[peer], dst_ref=halo.at[slot], send_sem=s3.at[i],
                    recv_sem=r3.at[source * NSEQ + i], device_id=target, device_id_type=MESH),
            )

        @pl.when(i > 0)
        def _():
            for copy in arrivals(branch):
                copy.wait_recv()

        for copy in arrivals(other):
            copy.wait_recv()
        return 0

    lax.fori_loop(0, NSEQ, wait_view, 0)

    listed = [jnp.where(is_time, time_blocks[0, n], freq_blocks[0, n]) for n in range(16)]

    def keep(q):
        block = me * BLOCKS + q
        hit = listed[0] == block
        for n in range(1, 16):
            hit = jnp.logical_or(hit, listed[n] == block)
        drop = jnp.logical_or(hit, jnp.logical_or(block < 0, block >= NSEQ * BLOCKS))
        return jnp.where(drop, 0.0, 1.0).astype(F32)

    for parity in range(2):
        tall[parity * 512:(parity + 1) * 512, :] = feat[:, parity].astype(F32).reshape(512, 128)
        for source in range(NPAIR * NSEQ):
            edges[parity * C + OWN * source:parity * C + OWN * (source + 1), :] = (
                halo[source, :, parity * 128:(parity + 1) * 128])
    side = lax.broadcasted_iota(jnp.int32, (128, 128), 1)
    rim = edges[...].astype(BF16).astype(F32) * jnp.where(side >= 64, keep(-1), keep(BLOCKS))
    wide[:, 0:128] = rim
    wide[:, 128 + PAIRS:256 + PAIRS] = rim
    rim_t = rim.T
    turned[0:8, :] = rim_t[120:128]
    turned[8 + PAIRS:16 + PAIRS, :] = rim_t[0:8]
    for q in range(BLOCKS):
        piece = tall[pl.ds(q, 128, stride=BLOCKS), :] * keep(q)
        wide[:, 128 * (q + 1):128 * (q + 2)] = piece
        turned[8 + 128 * q:8 + 128 * (q + 1), :] = piece.T
    across[...] = pltpu.roll(turned[...], 64, 1)
    low_half = lax.broadcasted_iota(jnp.int32, (ROWS, 128), 1) < 64
    for j in range(K // 2):
        columns = slice(128 * j, 128 * (j + 1))
        for r in range(PIECES):
            at = 8 + j - 2 + ROWS * r
            patches[r, 0:ROWS, columns] = turned[at:at + ROWS, :].astype(BF16)
            patches[r, ROWS:2 * ROWS, columns] = jnp.where(
                low_half, across[at:at + ROWS, :], across[at + 1:at + 1 + ROWS, :]).astype(BF16)
    for d in range(-2, 3):
        whole = wide[...]
        if d != 0:
            whole = pltpu.roll(whole, (-d) % (256 + PAIRS), 1)
        part = whole[:, 128:128 + PAIRS].astype(BF16)
        j = d + 2
        for r in range(PIECES):
            chunk = part[:, ROWS * r:ROWS * (r + 1)]
            at = 2 * ROWS * r
            if j < K // 2:
                patches_t[128 * j:128 * (j + 1), at:at + ROWS] = chunk
                patches_t[128 * j:128 * j + 64, at + ROWS:at + 2 * ROWS] = chunk[64:]
            if j > 0:
                patches_t[128 * (j - 1) + 64:128 * j, at + ROWS:at + 2 * ROWS] = chunk[:64]

    def encoded_copy(n):
        slot = lax.rem(n, 2)
        return pltpu.make_async_copy(
            held.at[slot],
            encoded.at[0, 0, :, pl.ds(pl.multiple_of(n * HB, HB), HB)], s_enc.at[slot])

    def core_copy(n):
        return pltpu.make_async_remote_copy(
            src_ref=grads.at[n, 1 - core], dst_ref=core_in.at[n], send_sem=s_core.at[n],
            recv_sem=r_core.at[n], device_id={"seq": sibling}, device_id_type=MESH)

    def chip_copy(n, i, slot):
        j = lax.rem(chip + i, CHIPS)
        return pltpu.make_async_remote_copy(
            src_ref=passed.at[n, j], dst_ref=chip_in.at[n, slot], send_sem=s_chip.at[n, i],
            recv_sem=r_chip.at[n, i], device_id={"seq": 2 * j + core}, device_id_type=MESH)

    def sum_copy(i, slot):
        return pltpu.make_async_remote_copy(
            src_ref=own_sum, dst_ref=all_sums.at[slot], send_sem=s_sum.at[i],
            recv_sem=r_sum.at[i], device_id={"seq": lax.rem(me + i, NSEQ)}, device_id_type=MESH)

    def pass_on(n):
        core_copy(n).wait_recv()

        def one(i, _):
            j = lax.rem(chip + i, CHIPS)
            passed[n, j] = grads[n, core, j] + core_in[n, j]
            chip_copy(n, i, chip).start()
            return 0

        lax.fori_loop(1, CHIPS, one, 0)

    def forward(n, _):
        weights = weight[0, pl.ds(pl.multiple_of(n * HB, HB), HB), :]

        @pl.when(n >= 2)
        def _():
            encoded_copy(n).wait()

        slot = lax.rem(n, 2)

        def product(r):
            return lax.dot_general(
                patches[r], weights, (((1,), (1,)), ((), ())), preferred_element_type=F32)

        count = jnp.zeros((8, HB), F32)
        kept = []
        preact = product(0)
        for r in range(PIECES):
            following = product(r + 1) if r + 1 < PIECES else None
            square = preact * preact
            inner = preact * (GELU_A + GELU_B * square)
            half = 0.5 * jnp.tanh(inner)
            gate = 0.5 + half
            active = preact * gate
            slope = gate + active * ((0.5 - half) * (2.0 * GELU_A + (6.0 * GELU_B) * square))
            pair = active[:ROWS] + active[ROWS:]
            held[slot, r * ROWS:(r + 1) * ROWS, :] = (pair * 0.5).astype(BF16)
            count = count + jnp.sum(pair.reshape(ROWS // 8, 8, HB), axis=0)
            kept.append(slope.astype(BF16))
            if len(kept) == DEPTH:
                at = 2 * ROWS * (r + 1 - DEPTH)
                update = jnp.dot(
                    patches_t[:, at:at + 2 * ROWS * DEPTH], jnp.concatenate(kept, axis=0),
                    preferred_element_type=F32)
                if r + 1 == DEPTH:
                    grad_t[...] = update
                else:
                    grad_t[...] += update
                kept = []
            preact = following
        total[n] = count
        encoded_copy(n).start()

        @pl.when(n == BANDS - 1)
        def _():
            for band in range(BANDS):
                own_sum[:, HB * band:HB * (band + 1)] = jnp.sum(
                    total[band], axis=0, keepdims=True)

            def start_sum(i, _):
                sum_copy(i, me).start()
                return 0

            lax.fori_loop(1, NSEQ, start_sum, 0)
            all_sums[me] = own_sum[...]

        grad = grad_t[...].T.reshape(2, CHIPS, 2, 8, K * C)
        for e in range(2):
            grads[n, e, :, 0:8, :] = grad[0, :, e]
            grads[n, e, :, 8:16, :] = grad[1, :, e]
        core_copy(n).start()

        @pl.when(n >= 1)
        def _():
            pass_on(n - 1)

        return 0

    lax.fori_loop(0, BANDS, forward, 0)

    def wait_sum(i, _):
        sum_copy(i, lax.rem(me - i + NSEQ, NSEQ)).wait_recv()
        return 0

    lax.fori_loop(1, NSEQ, wait_sum, 0)
    pooled = jnp.sum(all_sums[...], axis=0) * (1.0 / SEQLEN)
    latent = jnp.dot(
        jnp.broadcast_to(pooled, (8, H)), table[...], precision=HIGHEST,
        preferred_element_type=F32)[0:1]
    for g in range(NGRP):
        notes[g] = jnp.concatenate([latent, pooled[:, 128 * g:128 * (g + 1)]], axis=1)

    def own_copy(i, slot):
        peer = lax.rem(grp + i, NGRP)
        return pltpu.make_async_remote_copy(
            src_ref=notes.at[peer], dst_ref=own_notes.at[slot], send_sem=s_own.at[i],
            recv_sem=r_own.at[i], device_id={"grp": peer}, device_id_type=MESH)

    def other_copy(i, slot):
        peer = lax.rem(grp + i, NGRP)
        return pltpu.make_async_remote_copy(
            src_ref=notes.at[peer], dst_ref=other_notes.at[slot], send_sem=s_oth.at[i],
            recv_sem=r_oth.at[i], device_id={"pair": other, "grp": peer}, device_id_type=MESH)

    def start_notes(i, _):
        @pl.when(i > 0)
        def _():
            own_copy(i, grp).start()

        other_copy(i, grp).start()
        return 0

    lax.fori_loop(0, NGRP, start_notes, 0)
    own_notes[grp] = notes[grp]
    pass_on(BANDS - 1)

    def wait_notes(i, _):
        source = lax.rem(grp - i + NGRP, NGRP)

        @pl.when(i > 0)
        def _():
            own_copy(i, source).wait_recv()

        other_copy(i, source).wait_recv()
        return 0

    lax.fori_loop(0, NGRP, wait_notes, 0)
    for g in range(NGRP):
        own_rows[g:g + 1, :] = own_notes[g]
        other_rows[g:g + 1, :] = other_notes[g]
    z_own, z_other = own_rows[:, :E], other_rows[:, :E]
    scale = lax.rsqrt(jnp.sum(z_own * z_own, axis=1, keepdims=True) + 1e-06)
    scale_other = lax.rsqrt(jnp.sum(z_other * z_other, axis=1, keepdims=True) + 1e-06)
    e_own, e_other = z_own * scale, z_other * scale_other
    time_emb = jnp.where(is_time, e_own, e_other)
    freq_emb = jnp.where(is_time, e_other, e_own)
    dot = functools.partial(lax.dot_general, precision=HIGHEST, preferred_element_type=F32)
    logits = dot(time_emb, freq_emb, (((1,), (1,)), ((), ()))) * (1.0 / TAU)
    row = lax.broadcasted_iota(jnp.int32, (NGRP, NGRP), 0)
    col = lax.broadcasted_iota(jnp.int32, (NGRP, NGRP), 1)
    target = jnp.zeros((NGRP, NGRP), F32)
    for i in range(NGRP):
        target = jnp.where(jnp.logical_and(row == i, col == positives[i]), 1.0, target)
    exponent = jnp.exp(logits)
    by_row = jnp.sum(exponent, axis=1, keepdims=True)
    by_col = jnp.sum(exponent, axis=0, keepdims=True)
    slope = (exponent / by_row + exponent / by_col - 2.0 * target) * (
        LOSS_SCALE / (TAU * 2 * NGRP))
    d_time = dot(slope, freq_emb, (((1,), (0,)), ((), ())))
    d_freq = dot(slope, time_emb, (((0,), (0,)), ((), ())))
    d_emb = jnp.where(is_time, d_time, d_freq)
    along = jnp.sum(z_own * d_emb, axis=1, keepdims=True)
    d_latent = scale * d_emb - z_own * (scale * scale * scale * along)
    sample = lax.broadcasted_iota(jnp.int32, (NGRP, E), 0)
    d_mine = jnp.sum(jnp.where(sample == grp, d_latent, 0.0), axis=0, keepdims=True)

    def wait_chip(i, _):
        for n in range(BANDS):
            chip_copy(n, i, lax.rem(chip - i + CHIPS, CHIPS)).wait_recv()
        return 0

    lax.fori_loop(1, CHIPS, wait_chip, 0)
    for n in range(BANDS):
        chip_in[n, chip] = grads[n, core, chip] + core_in[n, chip]
        whole = chip_in[n, 0]
        for j in range(1, CHIPS):
            whole = whole + chip_in[n, j]
        for k in range(2):
            g = 2 * n + k
            at = pl.multiple_of(128 * g + 8 * me, 8)
            factor = jnp.sum(table[pl.ds(at, 8), :] * d_mine, axis=1, keepdims=True)
            ready[g] = whole[8 * k:8 * (k + 1)] * (factor * (1.0 / SEQLEN))

    def grp_copy(i, slot):
        peer = lax.rem(grp + i, NGRP)
        return pltpu.make_async_remote_copy(
            src_ref=ready.at[peer], dst_ref=grp_in.at[slot], send_sem=s_grp.at[i],
            recv_sem=r_grp.at[i], device_id={"grp": peer}, device_id_type=MESH)

    def start_grp(i, _):
        grp_copy(i, grp).start()
        return 0

    lax.fori_loop(1, NGRP, start_grp, 0)
    grp_in[grp] = ready[grp]

    picked = jnp.sum(jnp.sum(target * logits, axis=1, keepdims=True), axis=0, keepdims=True)
    lse = jnp.sum(jnp.log(by_row), axis=0, keepdims=True) + jnp.sum(
        jnp.log(by_col), axis=1, keepdims=True)
    loss_out[...] = (lse - 2.0 * picked) * (1.0 / (2 * NGRP))
    proj_out[0] = dot(own_rows[:, E:], d_latent, (((0,), (0,)), ((), ())))
    for n in range(BANDS - 2, BANDS):
        encoded_copy(n).wait()

    def sent_seq(i, _):
        for view, main, edge in ((0, time_main, time_halo), (1, freq_main, freq_halo)):
            @pl.when(jnp.logical_or(i > 0, branch != view))
            def _():
                for copy in view_copies(view, i, main, edge, mine):
                    copy.wait_send()

        @pl.when(i > 0)
        def _():
            series_copy(i, me).wait_send()
            sum_copy(i, me).wait_send()
        return 0

    def sent_grp(i, _):
        @pl.when(i > 0)
        def _():
            for n in range(BANDS):
                chip_copy(n, i, chip).wait_send()
            own_copy(i, grp).wait_send()
            grp_copy(i, grp).wait_send()

        other_copy(i, grp).wait_send()
        return 0

    lax.fori_loop(0, NSEQ, sent_seq, 0)
    for n in range(BANDS):
        core_copy(n).wait_send()

    def wait_grp(i, _):
        grp_copy(i, lax.rem(grp - i + NGRP, NGRP)).wait_recv()
        return 0

    lax.fori_loop(1, NGRP, wait_grp, 0)
    result = grp_in[0]
    for g in range(1, NGRP):
        result = result + grp_in[g]
    conv_out[0] = result
    lax.fori_loop(0, CHIPS, sent_grp, 0)


def body(series, time_blocks, freq_blocks, positives, conv_weight, proj_weight):
    vmem = pl.BlockSpec(memory_space=pltpu.VMEM)
    smem = pl.BlockSpec(memory_space=pltpu.SMEM)
    anywhere = pl.BlockSpec(memory_space=pltpu.HBM)
    tables = [jnp.asarray(t) for t in transform_tables()]
    sources = NPAIR * NSEQ
    dma = pltpu.SemaphoreType.DMA
    part = (BANDS, CHIPS, 16, K * C)
    main, edge = (NSEQ, 2, 16, 128), (NSEQ, OWN, 256)
    encoded, conv_share, proj_share, loss = pl.pallas_call(
        step_kernel,
        out_shape=(
            jax.ShapeDtypeStruct((1, 1, PAIRS, H), BF16),
            jax.ShapeDtypeStruct((1, 8, K * C), F32),
            jax.ShapeDtypeStruct((1, H // NGRP, E), F32),
            jax.ShapeDtypeStruct((1, 1), F32),
        ),
        in_specs=[smem] * 3 + [anywhere] * 9,
        out_specs=(anywhere, vmem, vmem, vmem),
        scratch_shapes=[
            pltpu.VMEM((OWN * NSEQ, SPAN), F32),
            pltpu.VMEM(conv_weight.shape, BF16),
            pltpu.VMEM(proj_weight.shape, BF16),
            *[pltpu.VMEM(t.shape, t.dtype) for t in tables],
            pltpu.VMEM((NSEQ * OWN * 16, 128), F32),
            pltpu.VMEM((NSEQ, OWN * 16, 128), F32),
            pltpu.VMEM((128, 128), F32),
            pltpu.VMEM(main, BF16),
            pltpu.VMEM(edge, F32),
            pltpu.VMEM(main, BF16),
            pltpu.VMEM(edge, F32),
            pltpu.VMEM((sources, 2, 16, 128), BF16),
            pltpu.VMEM((sources, OWN, 256), F32),
            pltpu.VMEM((8 * 2 * C, 128), F32),
            pltpu.VMEM((2 * C, 128), F32),
            pltpu.VMEM((2 * C, 256 + PAIRS), F32),
            pltpu.VMEM((16 + PAIRS, 128), F32),
            pltpu.VMEM((16 + PAIRS, 128), F32),
            pltpu.VMEM((PIECES, 2 * ROWS, K * C), BF16),
            pltpu.VMEM((K * C, SPAN), BF16),
            pltpu.VMEM((2, PAIRS, HB), BF16),
            pltpu.VMEM((BANDS, 8, HB), F32),
            pltpu.VMEM((K * C, HB), F32),
            pltpu.VMEM((1, H), F32),
            pltpu.VMEM((NSEQ, 1, H), F32),
            pltpu.VMEM((NGRP, 1, 2 * E), F32),
            pltpu.VMEM((NGRP, 1, 2 * E), F32),
            pltpu.VMEM((NGRP, 1, 2 * E), F32),
            pltpu.VMEM((NGRP, 2 * E), F32),
            pltpu.VMEM((NGRP, 2 * E), F32),
            pltpu.VMEM((H, E), F32),
            pltpu.VMEM((BANDS, 2, CHIPS, 16, K * C), F32),
            pltpu.VMEM(part, F32),
            pltpu.VMEM(part, F32),
            pltpu.VMEM(part, F32),
            pltpu.VMEM((NGRP, 8, K * C), F32),
            pltpu.VMEM((NGRP, 8, K * C), F32),
            dma((9,)), dma((2,)),
            dma((NSEQ,)), dma((NSEQ,)),
            dma((sources,)), dma((sources,)), dma((sources,)), dma((sources,)),
            dma((NSEQ,)), dma((NSEQ,)),
            dma((NGRP,)), dma((NGRP,)),
            dma((NGRP,)), dma((NGRP,)),
            dma((BANDS,)), dma((BANDS,)),
            dma((BANDS, CHIPS)), dma((BANDS, CHIPS)),
            dma((NGRP,)), dma((NGRP,)),
        ],
        compiler_params=pltpu.CompilerParams(
            collective_id=0, has_side_effects=True, vmem_limit_bytes=48 * 1024 * 1024),
        name="step",
    )(*[
        pltpu.with_memory_space_constraint(x, pltpu.HBM)
        for x in (positives, time_blocks, freq_blocks, series[0].T, conv_weight, proj_weight, *tables)
    ])
    return (encoded, loss[0, 0], conv_share, proj_share)


def solution(mesh):
    in_specs = (
        P("grp", "seq", "pair"),
        P("grp", None),
        P("grp", None),
        P(),
        P("pair", None, None),
        P("pair", None, None),
    )
    out_specs = (
        P("pair", "grp", "seq", None),
        P(),
        P("pair", ("grp", "seq"), None),
        P("pair", "grp", None),
    )
    return jax.shard_map(body, mesh=mesh, in_specs=in_specs, out_specs=out_specs, check_vma=False)
```

time: 86.5 us -> 61.7 us (0.71)
  Pallas kernels: 75.2 us -> 56.7 us
  local copies, waits for them, and re-layouts: 8.51 us -> 2.56 us
    pallas_call x3 -> x1, Pallas kernels: 75.2 us -> 56.7 us  [body(): pl.pallas_call(step_kernel, out_shape=(jax.ShapeDtypeStruct((1, 1, PAIRS,...]
    unnamed x16 -> x3, local copies, waits for them, and re-layouts: 6.54 us -> 2.56 us
    reshape x2 -> x0, local copies, waits for them, and re-layouts: 1.98 us -> none  [make_views(): series[0].T.reshape(NSEQ, OWN, BLOCKS, 2, 128).transpose(0, 1, 3, 2, 4)]
where the time goes in v2:
time: 61.7 us; the launch traced here: 61.5 us
  Pallas kernels  56.7 us (92%)
  local copies, waits for them, and re-layouts  2.56 us (4%)
  between operations  2.33 us (4%)
    pallas_call x1, Pallas kernels, body(): pl.pallas_call(step_kernel, out_shape=(jax.ShapeDtypeStruct((1, 1, PAIRS,...  56.7 us
    unnamed x3, local copies, waits for them, and re-layouts  2.56 us

profile of v2, /device:TPU:1, one launch (start us, length us, event | category | flops | bytes accessed | tf_op | source)
XLA Modules:
  0.0 61.5 jit_solution(11374351740873846820)
XLA Ops:
  0.6 56.7 %step.1 = (bf16[1,1,1024,1024]{3,2,1,0:T(8,128)(2,1)S(1)}, f32[1,8,512]{2,1,0:T(8,128)S(1)}, f32[1,128,128]{2,1,0:T(8,128)S(1)}, f32[1,1]{1,0:T(1,128)}) custom-call(s32[8]{0:T(128)} %positives.1, s32[1,16]{1,0:T(1,128)} %time_blocks.1, s32[1,16]{1,0:T(1,128)} %freq_blocks.1, f32[32,2048]{1,0:T(8,128)} %bitcast.4, bf16[1,1024,512]{2,1,0:T(8,128)(2,1)} %weight_in.1, ...), custom_call_target="tpu_custom_call" | custom-call | tf_op jit(solution)/shard_map/step/pallas_call | solution.py:574
  57.3 1.3 %copy.20 = bf16[1,1,1024,1024]{3,2,1,0:T(8,128)(2,1)} copy(bf16[1,1,1024,1024]{3,2,1,0:T(8,128)(2,1)S(1)} %get-tuple-element.16) | data formatting | bytes 4194304
  59.2 0.6 copy.22
  59.8 0.6 %copy.23 = f32[1,128,128]{2,1,0:T(8,128)} copy(f32[1,128,128]{2,1,0:T(8,128)S(1)} %get-tuple-element.19) | data formatting | bytes 131072

commit v3 on v2

--- a/solution.py
+++ b/solution.py
@@ -35,6 +35,8 @@
 BANDS = H // HB
 ROWS = 128
 PIECES = PAIRS // ROWS
+FLAT_FROM = 3.4
+STRIP = 16
 DEPTH = 2
 
 
@@ -62,19 +64,23 @@
     for odd_row in range(2):
         for step in range(128):
             pick[odd_row, step, 128 * (step % 2) + 64 * odd_row + step // 2] = 1.0
-    return (*split(first), turn, *split(second), pick.astype(BF16))
-
-
-def dot3(a, b_high, b_low, a_low=None):
-    dot = functools.partial(jnp.dot, preferred_element_type=F32)
-    return dot(a, b_high) + (dot(a, b_low) + dot(a_low, b_high))
+    return (*split(first), turn, np.concatenate(split(second), axis=0), pick.astype(BF16))
+
+
+def halves(values):
+    high = values.astype(BF16)
+    return high, (values - high.astype(F32)).astype(BF16)
+
+
+def mul(a, b):
+    return jnp.dot(a, b, preferred_element_type=F32)
 
 
 def step_kernel(
-    positives, time_blocks, freq_blocks, series_in, weight_in, proj_in,
-    first_h_in, first_l_in, turn_in, second_h_in, second_l_in, pick_in,
+    positives_in, time_blocks_in, freq_blocks_in, series_in, weight_in, proj_in,
+    first_h_in, first_l_in, turn_in, second_in, pick_in,
     encoded, conv_out, proj_out, loss_out,
-    raw, weight, proj, first_h, first_l, turn, second_h, second_l, pick,
+    positives, time_blocks, freq_blocks, raw, weight, proj, first_h, first_l, turn, second, pick,
     send, series, rows, time_main, time_halo, freq_main, freq_halo, feat, halo,
     tall, edges, wide, turned, across, patches, patches_t, held, total, grad_t,
     own_sum, all_sums, notes, own_notes, other_notes, own_rows, other_rows, table,
@@ -94,11 +100,12 @@
         pltpu.make_async_copy(src, dst, s_in.at[n])
         for n, (src, dst) in enumerate((
             (series_in, raw), (pick_in, pick), (first_h_in, first_h), (first_l_in, first_l),
-            (turn_in, turn), (second_h_in, second_h), (second_l_in, second_l),
-            (weight_in, weight), (proj_in, proj)))
+            (turn_in, turn), (second_in, second),
+            *[(weight_in.at[0, :, 128 * j:128 * (j + 1)], weight.at[j]) for j in range(K // 2)],
+            (proj_in.at[0], proj), (positives_in, positives), (time_blocks_in, time_blocks),
+            (freq_blocks_in, freq_blocks)))
     ]
-    for load in loads:
-        load.start()
+    loads[0].start()
 
     barrier = pltpu.get_barrier_semaphore()
 
@@ -120,6 +127,8 @@
 
     lax.fori_loop(0, NSEQ, greet_seq, 0)
     lax.fori_loop(1, NGRP, greet_grp, 0)
+    for load in loads[1:]:
+        load.start()
 
     loads[0].wait()
     for q in range(BLOCKS):
@@ -142,7 +151,7 @@
     series[me] = send[pl.ds(pl.multiple_of(32 * me, 32), 32), :]
     for load in loads[1:]:
         load.wait()
-    table[...] = proj[0].astype(F32)
+    table[...] = proj[pl.ds(pl.multiple_of(128 * grp, 128), 128), :].astype(F32)
 
     def wait_series(i, _):
         series_copy(i, lax.rem(me - i + NSEQ, NSEQ)).wait_recv()
@@ -199,6 +208,27 @@
             feat[mine] = main[me]
             halo[mine] = edge[me]
 
+    flats = []
+    for c in range(OWN):
+        whole = series[:, 16 * c:16 * c + 16, :].reshape(256, 128)
+        flats.append(jnp.concatenate([whole[:128].T, whole[128:].T], axis=1))
+    high, low = halves(jnp.concatenate(flats, axis=0))
+    part = mul(high, first_h[...]) + (mul(high, first_l[...]) + mul(low, first_h[...]))
+    re, im = part[:, :256], part[:, 256:]
+    cos = jnp.concatenate([turn[:, :256]] * OWN, axis=0)
+    sin = jnp.concatenate([turn[:, 256:]] * OWN, axis=0)
+    spun_re, spun_im = re * cos + im * sin, im * cos - re * sin
+    powers = []
+    for c in range(OWN):
+        at = slice(128 * c, 128 * (c + 1))
+        high, low = halves(jnp.concatenate([spun_re[at], spun_im[at]], axis=0))
+        both = mul(second[...], high)
+        spec = both[:256] + (both[256:] + mul(second[:256, :], low))
+        re, im = spec[:128], spec[128:]
+        powers.append(jnp.sqrt(1.0 + (re * re + im * im) * (1.0 / SEQLEN)))
+    pack(powers, freq_main, freq_halo)
+    start_view(1, freq_main, freq_halo)
+
     even = [series[:, 16 * c:16 * c + 8, :].reshape(128, 128) for c in range(OWN)]
     odd = [series[:, 16 * c + 8:16 * c + 16, :].reshape(128, 128) for c in range(OWN)]
     views = [
@@ -208,27 +238,6 @@
     ]
     pack(views, time_main, time_halo)
     start_view(0, time_main, time_halo)
-
-    spun = []
-    for c in range(OWN):
-        whole = series[:, 16 * c:16 * c + 16, :].reshape(256, 128)
-        flat = jnp.concatenate([whole[:128].T, whole[128:].T], axis=1)
-        high = flat.astype(BF16)
-        low = (flat - high.astype(F32)).astype(BF16)
-        part = dot3(high, first_h[...], first_l[...], low)
-        re, im = part[:, :256], part[:, 256:]
-        cos, sin = turn[:, :256], turn[:, 256:]
-        spun.append(jnp.concatenate([re * cos + im * sin, im * cos - re * sin], axis=0))
-    powers = []
-    for c in range(OWN):
-        high = spun[c].astype(BF16)
-        low = (spun[c] - high.astype(F32)).astype(BF16)
-        dot = functools.partial(jnp.dot, preferred_element_type=F32)
-        spec = dot(second_h[...], high) + (dot(second_h[...], low) + dot(second_l[...], high))
-        re, im = spec[:128], spec[128:]
-        powers.append(jnp.sqrt(1.0 + (re * re + im * im) * (1.0 / SEQLEN)))
-    pack(powers, freq_main, freq_halo)
-    start_view(1, freq_main, freq_halo)
 
     def wait_view(i, _):
         peer = lax.rem(me - i + NSEQ, NSEQ)
@@ -285,11 +294,10 @@
     across[...] = pltpu.roll(turned[...], 64, 1)
     low_half = lax.broadcasted_iota(jnp.int32, (ROWS, 128), 1) < 64
     for j in range(K // 2):
-        columns = slice(128 * j, 128 * (j + 1))
         for r in range(PIECES):
             at = 8 + j - 2 + ROWS * r
-            patches[r, 0:ROWS, columns] = turned[at:at + ROWS, :].astype(BF16)
-            patches[r, ROWS:2 * ROWS, columns] = jnp.where(
+            patches[r, j, 0:ROWS, :] = turned[at:at + ROWS, :].astype(BF16)
+            patches[r, j, ROWS:2 * ROWS, :] = jnp.where(
                 low_half, across[at:at + ROWS, :], across[at + 1:at + 1 + ROWS, :]).astype(BF16)
     for d in range(-2, 3):
         whole = wide[...]
@@ -299,18 +307,21 @@
         j = d + 2
         for r in range(PIECES):
             chunk = part[:, ROWS * r:ROWS * (r + 1)]
-            at = 2 * ROWS * r
             if j < K // 2:
-                patches_t[128 * j:128 * (j + 1), at:at + ROWS] = chunk
-                patches_t[128 * j:128 * j + 64, at + ROWS:at + 2 * ROWS] = chunk[64:]
+                patches_t[2 * r, 128 * j:128 * (j + 1), :] = chunk
+                patches_t[2 * r + 1, 128 * j:128 * j + 64, :] = chunk[64:]
             if j > 0:
-                patches_t[128 * (j - 1) + 64:128 * j, at + ROWS:at + 2 * ROWS] = chunk[:64]
-
-    def encoded_copy(n):
+                patches_t[2 * r + 1, 128 * (j - 1) + 64:128 * j, :] = chunk[:64]
+
+    def encoded_copies(n):
         slot = lax.rem(n, 2)
-        return pltpu.make_async_copy(
-            held.at[slot],
-            encoded.at[0, 0, :, pl.ds(pl.multiple_of(n * HB, HB), HB)], s_enc.at[slot])
+        return [
+            pltpu.make_async_copy(
+                held.at[slot, k],
+                encoded.at[0, 0, :, pl.ds(pl.multiple_of(n * HB + 128 * k, 128), 128)],
+                s_enc.at[slot, k])
+            for k in range(HB // 128)
+        ]
 
     def core_copy(n):
         return pltpu.make_async_remote_copy(
@@ -340,52 +351,71 @@
         lax.fori_loop(1, CHIPS, one, 0)
 
     def forward(n, _):
-        weights = weight[0, pl.ds(pl.multiple_of(n * HB, HB), HB), :]
+        at = pl.ds(pl.multiple_of(n * HB, HB), HB)
+        weights = jnp.concatenate([weight[j, at, :] for j in range(K // 2)], axis=1)
 
         @pl.when(n >= 2)
         def _():
-            encoded_copy(n).wait()
+            for copy in encoded_copies(n):
+                copy.wait()
 
         slot = lax.rem(n, 2)
 
         def product(r):
+            rows = jnp.concatenate([patches[r, j] for j in range(K // 2)], axis=1)
             return lax.dot_general(
-                patches[r], weights, (((1,), (1,)), ((), ())), preferred_element_type=F32)
-
-        count = jnp.zeros((8, HB), F32)
+                rows, weights, (((1,), (1,)), ((), ())), preferred_element_type=F32)
+
+        counts = [jnp.zeros((8, HB), F32)] * 3
         kept = []
         preact = product(0)
         for r in range(PIECES):
             following = product(r + 1) if r + 1 < PIECES else None
-            square = preact * preact
-            inner = preact * (GELU_A + GELU_B * square)
-            half = 0.5 * jnp.tanh(inner)
-            gate = 0.5 + half
-            active = preact * gate
-            slope = gate + active * ((0.5 - half) * (2.0 * GELU_A + (6.0 * GELU_B) * square))
-            pair = active[:ROWS] + active[ROWS:]
-            held[slot, r * ROWS:(r + 1) * ROWS, :] = (pair * 0.5).astype(BF16)
-            count = count + jnp.sum(pair.reshape(ROWS // 8, 8, HB), axis=0)
-            kept.append(slope.astype(BF16))
-            if len(kept) == DEPTH:
-                at = 2 * ROWS * (r + 1 - DEPTH)
-                update = jnp.dot(
-                    patches_t[:, at:at + 2 * ROWS * DEPTH], jnp.concatenate(kept, axis=0),
-                    preferred_element_type=F32)
+            firsts, seconds = [], []
+            for q in range(0, ROWS, STRIP):
+                slopes, active, flat = [], [], []
+                for base in (0, ROWS):
+                    value = preact[base + q:base + q + STRIP]
+                    square = value * value
+                    inner = value * (GELU_A + GELU_B * square)
+                    half = 0.5 * jnp.tanh(inner)
+                    gate = 0.5 + half
+                    active.append(value * gate)
+                    slopes.append(gate + active[-1] * (
+                        (0.5 - half) * (2.0 * GELU_A + (6.0 * GELU_B) * square)))
+                    flat.append(jnp.where(value > FLAT_FROM, 1.0, 0.0))
+                pair = active[0] + active[1]
+                mean = (pair * 0.5).astype(BF16)
+                for k in range(HB // 128):
+                    held[slot, k, r * ROWS + q:r * ROWS + q + STRIP, :] = (
+                        mean[:, 128 * k:128 * (k + 1)])
+                for k, both in enumerate((pair, flat[0] + flat[1], slopes[0] + slopes[1])):
+                    counts[k] = counts[k] + jnp.sum(both.reshape(STRIP // 8, 8, HB), axis=0)
+                firsts.append(slopes[0].astype(BF16))
+                seconds.append(slopes[1].astype(BF16))
+            kept.extend(firsts + seconds)
+            if (r + 1) % DEPTH == 0:
+                columns = range(2 * (r + 1 - DEPTH), 2 * (r + 1))
+                update = mul(
+                    jnp.concatenate([patches_t[k] for k in columns], axis=1),
+                    jnp.concatenate(kept, axis=0))
                 if r + 1 == DEPTH:
                     grad_t[...] = update
                 else:
                     grad_t[...] += update
                 kept = []
             preact = following
-        total[n] = count
-        encoded_copy(n).start()
+        for k in range(3):
+            total[n, k] = counts[k]
+        for copy in encoded_copies(n):
+            copy.start()
 
         @pl.when(n == BANDS - 1)
         def _():
             for band in range(BANDS):
-                own_sum[:, HB * band:HB * (band + 1)] = jnp.sum(
-                    total[band], axis=0, keepdims=True)
+                for k in range(3):
+                    at = H * k + HB * band
+                    own_sum[:, at:at + HB] = jnp.sum(total[band, k], axis=0, keepdims=True)
 
             def start_sum(i, _):
                 sum_copy(i, me).start()
@@ -413,12 +443,18 @@
         return 0
 
     lax.fori_loop(1, NSEQ, wait_sum, 0)
-    pooled = jnp.sum(all_sums[...], axis=0) * (1.0 / SEQLEN)
-    latent = jnp.dot(
-        jnp.broadcast_to(pooled, (8, H)), table[...], precision=HIGHEST,
-        preferred_element_type=F32)[0:1]
+    sums = jnp.sum(all_sums[...], axis=0)
+    pooled = sums[:, :H] * (1.0 / SEQLEN)
+    share = jnp.minimum(sums[:, H:2 * H] / jnp.maximum(sums[:, 2 * H:], 1.0), 1.0)
+    left, thirds = pooled, []
+    for _ in range(3):
+        thirds.append(left.astype(BF16).astype(F32))
+        left = left - thirds[-1]
+    thirds = jnp.concatenate(thirds + [jnp.zeros((5, H), F32)], axis=0).astype(BF16)
+    latent = jnp.sum(mul(thirds, proj[...]), axis=0, keepdims=True)
     for g in range(NGRP):
-        notes[g] = jnp.concatenate([latent, pooled[:, 128 * g:128 * (g + 1)]], axis=1)
+        at = slice(128 * g, 128 * (g + 1))
+        notes[g] = jnp.concatenate([latent, pooled[:, at], share[:, at]], axis=1)
 
     def own_copy(i, slot):
         peer = lax.rem(grp + i, NGRP)
@@ -443,6 +479,34 @@
     lax.fori_loop(0, NGRP, start_notes, 0)
     own_notes[grp] = notes[grp]
     pass_on(BANDS - 1)
+
+    def wait_chip(i, _):
+        for n in range(BANDS):
+            chip_copy(n, i, lax.rem(chip - i + CHIPS, CHIPS)).wait_recv()
+        return 0
+
+    lax.fori_loop(1, CHIPS, wait_chip, 0)
+    for n in range(BANDS):
+        chip_in[n, chip] = grads[n, core, chip] + core_in[n, chip]
+        whole = chip_in[n, 0]
+        for j in range(1, CHIPS):
+            whole = whole + chip_in[n, j]
+        for k in range(2):
+            g = 2 * n + k
+            ready[g] = whole[8 * k:8 * (k + 1)]
+
+    def grp_copy(i, slot):
+        peer = lax.rem(grp + i, NGRP)
+        return pltpu.make_async_remote_copy(
+            src_ref=ready.at[peer], dst_ref=grp_in.at[slot], send_sem=s_grp.at[i],
+            recv_sem=r_grp.at[i], device_id={"grp": peer}, device_id_type=MESH)
+
+    def start_grp(i, _):
+        grp_copy(i, grp).start()
+        return 0
+
+    lax.fori_loop(1, NGRP, start_grp, 0)
+    grp_in[grp] = ready[grp]
 
     def wait_notes(i, _):
         source = lax.rem(grp - i + NGRP, NGRP)
@@ -481,46 +545,33 @@
     d_emb = jnp.where(is_time, d_time, d_freq)
     along = jnp.sum(z_own * d_emb, axis=1, keepdims=True)
     d_latent = scale * d_emb - z_own * (scale * scale * scale * along)
-    sample = lax.broadcasted_iota(jnp.int32, (NGRP, E), 0)
-    d_mine = jnp.sum(jnp.where(sample == grp, d_latent, 0.0), axis=0, keepdims=True)
-
-    def wait_chip(i, _):
-        for n in range(BANDS):
-            chip_copy(n, i, lax.rem(chip - i + CHIPS, CHIPS)).wait_recv()
-        return 0
-
-    lax.fori_loop(1, CHIPS, wait_chip, 0)
-    for n in range(BANDS):
-        chip_in[n, chip] = grads[n, core, chip] + core_in[n, chip]
-        whole = chip_in[n, 0]
-        for j in range(1, CHIPS):
-            whole = whole + chip_in[n, j]
-        for k in range(2):
-            g = 2 * n + k
-            at = pl.multiple_of(128 * g + 8 * me, 8)
-            factor = jnp.sum(table[pl.ds(at, 8), :] * d_mine, axis=1, keepdims=True)
-            ready[g] = whole[8 * k:8 * (k + 1)] * (factor * (1.0 / SEQLEN))
-
-    def grp_copy(i, slot):
-        peer = lax.rem(grp + i, NGRP)
-        return pltpu.make_async_remote_copy(
-            src_ref=ready.at[peer], dst_ref=grp_in.at[slot], send_sem=s_grp.at[i],
-            recv_sem=r_grp.at[i], device_id={"grp": peer}, device_id_type=MESH)
-
-    def start_grp(i, _):
-        grp_copy(i, grp).start()
-        return 0
-
-    lax.fori_loop(1, NGRP, start_grp, 0)
-    grp_in[grp] = ready[grp]
+    own_proj = table[pl.ds(pl.multiple_of(8 * me, 8), 8), :] * (1.0 / SEQLEN)
+    take = jnp.where(
+        lax.broadcasted_iota(jnp.int32, (8, 128), 1)
+        == 8 * me + lax.broadcasted_iota(jnp.int32, (8, 128), 0), 1.0, 0.0)
+    shares = dot(take, own_rows[:, 2 * E:], (((1,), (1,)), ((), ())))
+    exact = jnp.concatenate([
+        jnp.sum(own_proj * d_latent[g:g + 1], axis=1, keepdims=True) for g in range(NGRP)], axis=1)
+    blend = exact + shares * (exact.astype(BF16).astype(F32) - exact)
+    factors = [blend[:, g:g + 1] for g in range(NGRP)]
 
     picked = jnp.sum(jnp.sum(target * logits, axis=1, keepdims=True), axis=0, keepdims=True)
     lse = jnp.sum(jnp.log(by_row), axis=0, keepdims=True) + jnp.sum(
         jnp.log(by_col), axis=1, keepdims=True)
     loss_out[...] = (lse - 2.0 * picked) * (1.0 / (2 * NGRP))
-    proj_out[0] = dot(own_rows[:, E:], d_latent, (((0,), (0,)), ((), ())))
+    proj_out[0] = dot(own_rows[:, E:2 * E], d_latent, (((0,), (0,)), ((), ())))
+    def wait_grp(i, _):
+        grp_copy(i, lax.rem(grp - i + NGRP, NGRP)).wait_recv()
+        return 0
+
+    lax.fori_loop(1, NGRP, wait_grp, 0)
+    result = grp_in[0] * factors[0]
+    for g in range(1, NGRP):
+        result = result + grp_in[g] * factors[g]
+    conv_out[0] = result
     for n in range(BANDS - 2, BANDS):
-        encoded_copy(n).wait()
+        for copy in encoded_copies(n):
+            copy.wait()
 
     def sent_seq(i, _):
         for view, main, edge in ((0, time_main, time_halo), (1, freq_main, freq_halo)):
@@ -550,22 +601,22 @@
     for n in range(BANDS):
         core_copy(n).wait_send()
 
-    def wait_grp(i, _):
-        grp_copy(i, lax.rem(grp - i + NGRP, NGRP)).wait_recv()
-        return 0
-
-    lax.fori_loop(1, NGRP, wait_grp, 0)
-    result = grp_in[0]
-    for g in range(1, NGRP):
-        result = result + grp_in[g]
-    conv_out[0] = result
     lax.fori_loop(0, CHIPS, sent_grp, 0)
+
+
+def finish_kernel(*refs):
+    sems = refs[8]
+    copies = [pltpu.make_async_copy(refs[n], refs[4 + n], sems.at[n]) for n in range(4)]
+    for copy in copies:
+        copy.start()
+    for copy in copies:
+        copy.wait()
 
 
 def body(series, time_blocks, freq_blocks, positives, conv_weight, proj_weight):
     vmem = pl.BlockSpec(memory_space=pltpu.VMEM)
-    smem = pl.BlockSpec(memory_space=pltpu.SMEM)
-    anywhere = pl.BlockSpec(memory_space=pltpu.HBM)
+    hbm = pl.BlockSpec(memory_space=pltpu.HBM)
+    anywhere = pl.BlockSpec(memory_space=pl.ANY)
     tables = [jnp.asarray(t) for t in transform_tables()]
     sources = NPAIR * NSEQ
     dma = pltpu.SemaphoreType.DMA
@@ -579,12 +630,15 @@
             jax.ShapeDtypeStruct((1, H // NGRP, E), F32),
             jax.ShapeDtypeStruct((1, 1), F32),
         ),
-        in_specs=[smem] * 3 + [anywhere] * 9,
+        in_specs=[hbm] * 11,
         out_specs=(anywhere, vmem, vmem, vmem),
         scratch_shapes=[
+            pltpu.SMEM((NGRP,), jnp.int32),
+            pltpu.SMEM((1, 16), jnp.int32),
+            pltpu.SMEM((1, 16), jnp.int32),
             pltpu.VMEM((OWN * NSEQ, SPAN), F32),
-            pltpu.VMEM(conv_weight.shape, BF16),
-            pltpu.VMEM(proj_weight.shape, BF16),
+            pltpu.VMEM((K // 2, H, 128), BF16),
+            pltpu.VMEM((H, E), BF16),
             *[pltpu.VMEM(t.shape, t.dtype) for t in tables],
             pltpu.VMEM((NSEQ * OWN * 16, 128), F32),
             pltpu.VMEM((NSEQ, OWN * 16, 128), F32),
@@ -600,26 +654,26 @@
             pltpu.VMEM((2 * C, 256 + PAIRS), F32),
             pltpu.VMEM((16 + PAIRS, 128), F32),
             pltpu.VMEM((16 + PAIRS, 128), F32),
-            pltpu.VMEM((PIECES, 2 * ROWS, K * C), BF16),
-            pltpu.VMEM((K * C, SPAN), BF16),
-            pltpu.VMEM((2, PAIRS, HB), BF16),
-            pltpu.VMEM((BANDS, 8, HB), F32),
+            pltpu.VMEM((PIECES, K // 2, 2 * ROWS, 128), BF16),
+            pltpu.VMEM((2 * PIECES, K * C, 128), BF16),
+            pltpu.VMEM((2, HB // 128, PAIRS, 128), BF16),
+            pltpu.VMEM((BANDS, 3, 8, HB), F32),
             pltpu.VMEM((K * C, HB), F32),
-            pltpu.VMEM((1, H), F32),
-            pltpu.VMEM((NSEQ, 1, H), F32),
-            pltpu.VMEM((NGRP, 1, 2 * E), F32),
-            pltpu.VMEM((NGRP, 1, 2 * E), F32),
-            pltpu.VMEM((NGRP, 1, 2 * E), F32),
-            pltpu.VMEM((NGRP, 2 * E), F32),
-            pltpu.VMEM((NGRP, 2 * E), F32),
-            pltpu.VMEM((H, E), F32),
+            pltpu.VMEM((1, 3 * H), F32),
+            pltpu.VMEM((NSEQ, 1, 3 * H), F32),
+            pltpu.VMEM((NGRP, 1, 3 * E), F32),
+            pltpu.VMEM((NGRP, 1, 3 * E), F32),
+            pltpu.VMEM((NGRP, 1, 3 * E), F32),
+            pltpu.VMEM((NGRP, 3 * E), F32),
+            pltpu.VMEM((NGRP, 3 * E), F32),
+            pltpu.VMEM((128, E), F32),
             pltpu.VMEM((BANDS, 2, CHIPS, 16, K * C), F32),
             pltpu.VMEM(part, F32),
             pltpu.VMEM(part, F32),
             pltpu.VMEM(part, F32),
             pltpu.VMEM((NGRP, 8, K * C), F32),
             pltpu.VMEM((NGRP, 8, K * C), F32),
-            dma((9,)), dma((2,)),
+            dma((14,)), dma((2, 2)),
             dma((NSEQ,)), dma((NSEQ,)),
             dma((sources,)), dma((sources,)), dma((sources,)), dma((sources,)),
             dma((NSEQ,)), dma((NSEQ,)),
@@ -636,6 +690,18 @@
         pltpu.with_memory_space_constraint(x, pltpu.HBM)
         for x in (positives, time_blocks, freq_blocks, series[0].T, conv_weight, proj_weight, *tables)
     ])
+    outs = [
+        pltpu.with_memory_space_constraint(x, pltpu.VMEM)
+        for x in (encoded, conv_share, proj_share, loss)
+    ]
+    encoded, conv_share, proj_share, loss = pl.pallas_call(
+        finish_kernel,
+        out_shape=[jax.ShapeDtypeStruct(x.shape, x.dtype) for x in outs],
+        in_specs=[pl.BlockSpec(memory_space=pltpu.VMEM)] * 4,
+        out_specs=[pl.BlockSpec(memory_space=pltpu.HBM)] * 4,
+        scratch_shapes=[dma((4,))],
+        name="finish",
+    )(*outs)
     return (encoded, loss[0, 0], conv_share, proj_share)
 
 

time: 61.7 us -> 58.9 us (0.955)
  local copies, waits for them, and re-layouts: 2.56 us -> 0 us
  between operations: 2.33 us -> 0.64 us
  Pallas kernels: 56.7 us -> 57.7 us
    unnamed x3 -> x0, local copies, waits for them, and re-layouts: 2.56 us -> none
    pallas_call x0 -> x1, Pallas kernels: none -> 1.99 us  [body(): pl.pallas_call(finish_kernel, out_shape=[jax.ShapeDtypeStruct(x.shape, x....]
    pallas_call x1, Pallas kernels: 56.7 us -> 55.7 us  [body(): pl.pallas_call(step_kernel, out_shape=(jax.ShapeDtypeStruct((1, 1, PAIRS,...]
where the time goes in v3:
time: 58.9 us; the launch traced here: 58.4 us
  Pallas kernels  57.7 us (98%)
  between operations  0.64 us (1%)
    pallas_call x1, Pallas kernels, body(): pl.pallas_call(step_kernel, out_shape=(jax.ShapeDtypeStruct((1, 1, PAIRS,...  55.7 us
    pallas_call x1, Pallas kernels, body(): pl.pallas_call(finish_kernel, out_shape=[jax.ShapeDtypeStruct(x.shape, x....  1.99 us

profile of v3, /device:TPU:1, one launch (start us, length us, event | category | flops | bytes accessed | tf_op | source)
XLA Modules:
  0.0 58.4 jit_solution(14834544058425755195)
XLA Ops:
  0.6 55.7 %step.1 = (bf16[1,1,1024,1024]{3,2,1,0:T(8,128)(2,1)S(1)}, f32[1,8,512]{2,1,0:T(8,128)S(1)}, f32[1,128,128]{2,1,0:T(8,128)S(1)}, f32[1,1]{1,0:T(1,128)}) custom-call(s32[8]{0:T(128)} %positives_in.1, s32[1,16]{1,0:T(1,128)} %time_blocks_in.1, s32[1,16]{1,0:T(1,128)} %freq_blocks_in.1, f32[32,2048]{1,0:T(8,128)} %bitcast.4, bf16[1,1024,512]{2,1,0:T(8,128)(2,1)} %weight_in.1, ...), custom_call_target="tpu_custom_call" | custom-call | tf_op jit(solution)/shard_map/step/pallas_call | solution.py:625
  56.4 2.0 %finish.1 = (bf16[1,1,1024,1024]{3,2,1,0:T(8,128)(2,1)}, f32[1,8,512]{2,1,0:T(8,128)}, f32[1,128,128]{2,1,0:T(8,128)}, f32[1,1]{1,0:T(1,128)}) custom-call(bf16[1,1,1024,1024]{3,2,1,0:T(8,128)(2,1)S(1)} %get-tuple-element.12.refs_0_, f32[1,8,512]{2,1,0:T(8,128)S(1)} %get-tuple-element.13.refs_1_, f32[1,128,128]{2,1,0:T(8,128)S(1)} %get-tuple-element.14.refs_2_, ...), custom_call_target="tpu_custom_call" | custom-call | tf_op jit(solution)/shard_map/finish/pallas_call | solution.py:697

commit v4 on v3

--- a/solution.py
+++ b/solution.py
@@ -438,10 +438,37 @@
 
     lax.fori_loop(0, BANDS, forward, 0)
 
+    def grp_copy(i, slot):
+        peer = lax.rem(grp + i, NGRP)
+        return pltpu.make_async_remote_copy(
+            src_ref=ready.at[peer], dst_ref=grp_in.at[slot], send_sem=s_grp.at[i],
+            recv_sem=r_grp.at[i], device_id={"grp": peer}, device_id_type=MESH)
+
+    def hand_over(n):
+        def wait_chip(i, _):
+            chip_copy(n, i, lax.rem(chip - i + CHIPS, CHIPS)).wait_recv()
+            return 0
+
+        lax.fori_loop(1, CHIPS, wait_chip, 0)
+        chip_in[n, chip] = grads[n, core, chip] + core_in[n, chip]
+        whole = chip_in[n, 0]
+        for j in range(1, CHIPS):
+            whole = whole + chip_in[n, j]
+        for k in range(2):
+            g = 2 * n + k
+            ready[g] = whole[8 * k:8 * (k + 1)]
+            i = lax.rem(g - grp + NGRP, NGRP)
+
+            @pl.when(i > 0)
+            def _():
+                grp_copy(i, grp).start()
+
     def wait_sum(i, _):
         sum_copy(i, lax.rem(me - i + NSEQ, NSEQ)).wait_recv()
         return 0
 
+    pass_on(BANDS - 1)
+    hand_over(0)
     lax.fori_loop(1, NSEQ, wait_sum, 0)
     sums = jnp.sum(all_sums[...], axis=0)
     pooled = sums[:, :H] * (1.0 / SEQLEN)
@@ -478,34 +505,9 @@
 
     lax.fori_loop(0, NGRP, start_notes, 0)
     own_notes[grp] = notes[grp]
-    pass_on(BANDS - 1)
-
-    def wait_chip(i, _):
-        for n in range(BANDS):
-            chip_copy(n, i, lax.rem(chip - i + CHIPS, CHIPS)).wait_recv()
-        return 0
-
-    lax.fori_loop(1, CHIPS, wait_chip, 0)
-    for n in range(BANDS):
-        chip_in[n, chip] = grads[n, core, chip] + core_in[n, chip]
-        whole = chip_in[n, 0]
-        for j in range(1, CHIPS):
-            whole = whole + chip_in[n, j]
-        for k in range(2):
-            g = 2 * n + k
-            ready[g] = whole[8 * k:8 * (k + 1)]
-
-    def grp_copy(i, slot):
-        peer = lax.rem(grp + i, NGRP)
-        return pltpu.make_async_remote_copy(
-            src_ref=ready.at[peer], dst_ref=grp_in.at[slot], send_sem=s_grp.at[i],
-            recv_sem=r_grp.at[i], device_id={"grp": peer}, device_id_type=MESH)
-
-    def start_grp(i, _):
-        grp_copy(i, grp).start()
-        return 0
-
-    lax.fori_loop(1, NGRP, start_grp, 0)
+
+    for n in range(1, BANDS):
+        hand_over(n)
     grp_in[grp] = ready[grp]
 
     def wait_notes(i, _):

time: 58.9 us -> 55.5 us (0.942)
  Pallas kernels: 57.7 us -> 54.8 us
    pallas_call x1, Pallas kernels: 55.7 us -> 52.8 us  [body(): pl.pallas_call(step_kernel, out_shape=(jax.ShapeDtypeStruct((1, 1, PAIRS,...]
where the time goes in v4:
time: 55.5 us; the launch traced here: 55.4 us
  Pallas kernels  54.8 us (99%)
  between operations  0.64 us (1%)
    pallas_call x1, Pallas kernels, body(): pl.pallas_call(step_kernel, out_shape=(jax.ShapeDtypeStruct((1, 1, PAIRS,...  52.8 us
    pallas_call x1, Pallas kernels, body(): pl.pallas_call(finish_kernel, out_shape=[jax.ShapeDtypeStruct(x.shape, x....  1.99 us

profile of v4, /device:TPU:1, one launch (start us, length us, event | category | flops | bytes accessed | tf_op | source)
XLA Modules:
  0.0 55.4 jit_solution(9147575015864969496)
XLA Ops:
  0.6 52.8 %step.1 = (bf16[1,1,1024,1024]{3,2,1,0:T(8,128)(2,1)S(1)}, f32[1,8,512]{2,1,0:T(8,128)S(1)}, f32[1,128,128]{2,1,0:T(8,128)S(1)}, f32[1,1]{1,0:T(1,128)}) custom-call(s32[8]{0:T(128)} %positives_in.1, s32[1,16]{1,0:T(1,128)} %time_blocks_in.1, s32[1,16]{1,0:T(1,128)} %freq_blocks_in.1, f32[32,2048]{1,0:T(8,128)} %bitcast.4, bf16[1,1024,512]{2,1,0:T(8,128)(2,1)} %weight_in.1, ...), custom_call_target="tpu_custom_call" | custom-call | tf_op jit(solution)/shard_map/step/pallas_call | solution.py:627
  53.4 2.0 %finish.1 = (bf16[1,1,1024,1024]{3,2,1,0:T(8,128)(2,1)}, f32[1,8,512]{2,1,0:T(8,128)}, f32[1,128,128]{2,1,0:T(8,128)}, f32[1,1]{1,0:T(1,128)}) custom-call(bf16[1,1,1024,1024]{3,2,1,0:T(8,128)(2,1)S(1)} %get-tuple-element.12.refs_0_, f32[1,8,512]{2,1,0:T(8,128)S(1)} %get-tuple-element.13.refs_1_, f32[1,128,128]{2,1,0:T(8,128)S(1)} %get-tuple-element.14.refs_2_, ...), custom_call_target="tpu_custom_call" | custom-call | tf_op jit(solution)/shard_map/finish/pallas_call | solution.py:699

commit v5 on v4

--- a/solution.py
+++ b/solution.py
@@ -37,7 +37,7 @@
 PIECES = PAIRS // ROWS
 FLAT_FROM = 3.4
 STRIP = 16
-DEPTH = 2
+DEPTH = 1
 
 
 def split(values):

time: 55.5 us -> 54.4 us (0.980)
  Pallas kernels: 54.8 us -> 53.6 us
    pallas_call x1, Pallas kernels: 52.8 us -> 51.6 us  [body(): pl.pallas_call(step_kernel, out_shape=(jax.ShapeDtypeStruct((1, 1, PAIRS,...]
where the time goes in v5:
time: 54.4 us; the launch traced here: 54.2 us
  Pallas kernels  53.6 us (99%)
  between operations  0.64 us (1%)
    pallas_call x1, Pallas kernels, body(): pl.pallas_call(step_kernel, out_shape=(jax.ShapeDtypeStruct((1, 1, PAIRS,...  51.6 us
    pallas_call x1, Pallas kernels, body(): pl.pallas_call(finish_kernel, out_shape=[jax.ShapeDtypeStruct(x.shape, x....  1.99 us

profile of v5, /device:TPU:1, one launch (start us, length us, event | category | flops | bytes accessed | tf_op | source)
XLA Modules:
  0.0 54.2 jit_solution(6743426974770350460)
XLA Ops:
  0.6 51.6 %step.1 = (bf16[1,1,1024,1024]{3,2,1,0:T(8,128)(2,1)S(1)}, f32[1,8,512]{2,1,0:T(8,128)S(1)}, f32[1,128,128]{2,1,0:T(8,128)S(1)}, f32[1,1]{1,0:T(1,128)}) custom-call(s32[8]{0:T(128)} %positives_in.1, s32[1,16]{1,0:T(1,128)} %time_blocks_in.1, s32[1,16]{1,0:T(1,128)} %freq_blocks_in.1, f32[32,2048]{1,0:T(8,128)} %bitcast.4, bf16[1,1024,512]{2,1,0:T(8,128)(2,1)} %weight_in.1, ...), custom_call_target="tpu_custom_call" | custom-call | tf_op jit(solution)/shard_map/step/pallas_call | solution.py:627
  52.2 2.0 %finish.1 = (bf16[1,1,1024,1024]{3,2,1,0:T(8,128)(2,1)}, f32[1,8,512]{2,1,0:T(8,128)}, f32[1,128,128]{2,1,0:T(8,128)}, f32[1,1]{1,0:T(1,128)}) custom-call(bf16[1,1,1024,1024]{3,2,1,0:T(8,128)(2,1)S(1)} %get-tuple-element.12.refs_0_, f32[1,8,512]{2,1,0:T(8,128)S(1)} %get-tuple-element.13.refs_1_, f32[1,128,128]{2,1,0:T(8,128)S(1)} %get-tuple-element.14.refs_2_, ...), custom_call_target="tpu_custom_call" | custom-call | tf_op jit(solution)/shard_map/finish/pallas_call | solution.py:699
